TPU v7x, 32 devices: a whole 2x2x4 slice. The times are simulated.
32 devices in a mesh: mem: 4 (over x, core), expert: 8 (over z, y).
Axes of the slice: x: 2, y: 2, z: 4, core: 2. Of those that a mesh axis runs over, the one named last changes fastest.
Arguments:
- queries: bfloat16 [8192, 4096], P(('mem', 'expert')), may hold values from -128 to 128
- out_grad: bfloat16 [8192, 4096], P(('mem', 'expert')), may hold values from -12 to 12
- mem_keys: bfloat16 [4096, 4096], P('mem', 'expert'), may hold values from -4.5 to 4.5
- mem_values: bfloat16 [4096, 4096], P('mem', 'expert'), may hold values from -48 to 48
- block_index: int32 [64, 4], P('mem'), may hold values from 0 to 31, as said below
- routes: int32 [8192, 2], P(('mem', 'expert')), may hold values from 0 to 7, all different within a row; in each aligned block of 256 rows (0 to 255, 256 to 511, ...) at most 96 rows name the same one
- combine: bfloat16 [8192, 2], P(('mem', 'expert')), may hold values from 0.049804688 to 1
- gate_pre: bfloat16 [8, 3072, 768], P('expert', 'mem'), may hold values from -6 to 6
- up_pre: bfloat16 [8, 3072, 768], P('expert', 'mem'), may hold values from -6 to 6
- w_down: bfloat16 [8, 768, 4096], P('expert', 'mem'), may hold values from -0.21875 to 0.21875
Outputs:
- query_grad: bfloat16 [8192, 4096], P('mem', 'expert')
- w_down_grad: bfloat16 [8, 768, 4096], P('expert', 'mem')
- gate_grad: bfloat16 [8, 3072, 768], P('expert', 'mem')
- up_grad: bfloat16 [8, 3072, 768], P('expert', 'mem')
- combine_grad: float32 [8, 3072], P('expert', 'mem')
Inputs may be any that keep to these rules, and one draw needn't show every extreme that they name: `block_index`: each row names 4 memory blocks of 4 different owner groups, where block c belongs to group c // 8. `routes`: each row names 2 different experts; within the 256 rows of one device no expert is named by more than 96 rows, a bound that some block reaches.
All inputs are finite; a program needn't handle non-finite values.
Results may differ from a plain program's by a relative error of at most 0.013.
Values may be sent and summed in bfloat16 or wider, within the bound.
A program may use at most 192 MiB of HBM per device.

v0:
```python
import jax
import jax.numpy as jnp
from jax import lax
from jax.sharding import PartitionSpec as P

HD = 128
QBLK = 128


NEG_FILL = -1e30


def pick_blocks(source_rows, chosen):
    block_count = source_rows.shape[0] // QBLK
    inside = (chosen >= 0) & (chosen < block_count)
    clipped = jnp.clip(chosen, 0, block_count - 1)
    blocks = jnp.take(source_rows.reshape(block_count, QBLK, source_rows.shape[1]), clipped, axis=0)
    batch_size = chosen.shape[0]
    picked = blocks.reshape(batch_size, chosen.shape[1] * QBLK, source_rows.shape[1] // HD, HD)
    visible = jnp.repeat(inside, QBLK, axis=1)[:, None, None, :]
    return (picked, visible)


def owned_slots(block_index, first_block, block_count):
    inside = ((block_index >= first_block) & (block_index < first_block + block_count)).astype(
        jnp.int32
    )
    order = jnp.argsort(1 - inside, axis=1, stable=True)
    return jnp.take_along_axis(block_index, order, axis=1)


def per_device(
    queries, out_grad, mem_keys, mem_values, block_index, routes, combine, gate_pre, up_pre, w_down
):
    experts = lax.axis_size("expert")
    tok_count, model_width = out_grad.shape
    capacity = gate_pre.shape[1] // experts
    expert_ids = jnp.arange(experts, dtype=jnp.int32)
    route_hits = (routes[:, :, None] == expert_ids[None, None, :]).astype(jnp.int32)
    named_count = jnp.sum(route_hits, axis=1, dtype=jnp.int32)
    before = jnp.cumsum(named_count, axis=0, dtype=jnp.int32) - named_count
    placing = (before.T[None, :, :] == jnp.arange(capacity, dtype=jnp.int32)[:, None, None]) & (
        named_count.T[None, :, :] > 0
    )
    placing_mat = placing.astype(jnp.bfloat16).reshape(capacity * experts, tok_count)
    slot_rows = (
        jnp.dot(placing_mat, out_grad, preferred_element_type=jnp.float32)
        .astype(jnp.bfloat16)
        .reshape(capacity, experts * model_width)
    )
    token_weight = jnp.sum(
        route_hits.astype(jnp.float32) * combine.astype(jnp.float32)[:, :, None], axis=1
    )
    slot_weight = jnp.sum(placing.astype(jnp.float32) * token_weight.T[None, :, :], axis=2).astype(
        jnp.bfloat16
    )
    head_queries, head_grads, expert_rows, expert_weight = (
        lax.all_to_all(queries, "expert", split_axis=1, concat_axis=0, tiled=True),
        lax.all_to_all(out_grad, "expert", split_axis=1, concat_axis=0, tiled=True),
        lax.all_to_all(slot_rows, "expert", split_axis=1, concat_axis=0, tiled=True),
        lax.all_to_all(slot_weight, "expert", split_axis=1, concat_axis=0, tiled=True),
    )
    weight_col = expert_weight[:, 0].astype(jnp.float32)
    back_grad = lax.dot_general(
        expert_rows,
        lax.all_gather(w_down, "mem", axis=1, tiled=True)[0],
        (((1,), (1,)), ((), ())),
        preferred_element_type=jnp.float32,
    )
    gate_val = gate_pre[0].astype(jnp.float32)
    up_val = up_pre[0].astype(jnp.float32)
    sigmoid_gate = jax.nn.sigmoid(gate_val)
    silu_gate = gate_val * sigmoid_gate
    hidden = silu_gate * up_val
    combine_grad = jnp.sum(hidden * back_grad, axis=-1)[None]
    hidden_grad = weight_col[:, None] * back_grad
    gate_grad = (
        hidden_grad * up_val * sigmoid_gate * (1.0 + gate_val * (1.0 - sigmoid_gate))
    ).astype(jnp.bfloat16)[None]
    up_grad = (hidden_grad * silu_gate).astype(jnp.bfloat16)[None]
    weighted = (weight_col[:, None] * hidden).astype(jnp.bfloat16)
    w_down_grad = lax.psum_scatter(
        lax.dot_general(
            weighted, expert_rows, (((0,), (0,)), ((), ())), preferred_element_type=jnp.float32
        ).astype(jnp.bfloat16),
        "mem",
        scatter_dimension=0,
        tiled=True,
    )[None]
    row_count, head_cols = head_queries.shape
    heads_here = head_cols // HD
    batch_blocks = row_count // QBLK
    query_blocks = head_queries.reshape(batch_blocks, QBLK, heads_here, HD)
    grad_blocks = head_grads.reshape(batch_blocks, QBLK, heads_here, HD)
    score_scale = 1.0 / HD**0.5

    def piece_blocks(pieces, piece_start):
        first_block = piece_start // QBLK
        block_count = pieces[0].shape[0] // QBLK
        chosen = owned_slots(block_index, first_block, block_count)
        picked_keys, visible = pick_blocks(pieces[0], chosen)
        picked_values = pick_blocks(pieces[1], chosen)[0]
        return (picked_keys, picked_values, visible)

    start_shape = (batch_blocks, heads_here, QBLK)
    gather_highest = jnp.full(start_shape, NEG_FILL, jnp.float32)
    picked_keys, picked_values, visible = piece_blocks(
        (
            lax.all_gather(mem_keys, "mem", axis=0, tiled=True),
            lax.all_gather(mem_values, "mem", axis=0, tiled=True),
        ),
        jnp.int32(0),
    )
    scores = (
        jnp.einsum("bqhd,bkhd->bhqk", query_blocks, picked_keys, preferred_element_type=jnp.float32)
        * score_scale
    )
    scores = jnp.where(visible, scores, NEG_FILL)
    raised = jnp.maximum(gather_highest, jnp.max(scores, axis=-1))
    weights = jnp.where(visible, jnp.exp(scores - raised[..., None]), 0.0)
    grad_probs = jnp.einsum(
        "bqhd,bkhd->bhqk", grad_blocks, picked_values, preferred_element_type=jnp.float32
    )
    row_total = jnp.sum(weights, axis=-1)
    cross_sum = jnp.sum(weights * grad_probs, axis=-1)
    delta_sum = (cross_sum / row_total)[..., None]
    picked_keys, picked_values, visible = piece_blocks(
        (
            lax.all_gather(mem_keys, "mem", axis=0, tiled=True),
            lax.all_gather(mem_values, "mem", axis=0, tiled=True),
        ),
        jnp.int32(0),
    )
    scores = (
        jnp.einsum("bqhd,bkhd->bhqk", query_blocks, picked_keys, preferred_element_type=jnp.float32)
        * score_scale
    )
    probabilities = jnp.where(
        visible, jnp.exp(scores - raised[..., None]) / row_total[..., None], 0.0
    )
    grad_probs = jnp.einsum(
        "bqhd,bkhd->bhqk", grad_blocks, picked_values, preferred_element_type=jnp.float32
    )
    grad_scores = (probabilities * (grad_probs - delta_sum)).astype(jnp.bfloat16)
    query_total = jnp.einsum(
        "bhqk,bkhd->bqhd", grad_scores, picked_keys, preferred_element_type=jnp.float32
    )
    query_grad = (query_total * score_scale).astype(jnp.bfloat16).reshape(row_count, head_cols)
    return (query_grad, w_down_grad, gate_grad, up_grad, combine_grad)


def solution(mesh):
    in_specs = (
        P(("mem", "expert"), None),
        P(("mem", "expert"), None),
        P("mem", "expert"),
        P("mem", "expert"),
        P("mem", None),
        P(("mem", "expert"), None),
        P(("mem", "expert"), None),
        P("expert", "mem", None),
        P("expert", "mem", None),
        P("expert", "mem", None),
    )
    out_specs = (
        P("mem", "expert"),
        P("expert", "mem", None),
        P("expert", "mem", None),
        P("expert", "mem", None),
        P("expert", "mem"),
    )
    return jax.shard_map(
        per_device, mesh=mesh, in_specs=in_specs, out_specs=out_specs, check_vma=False
    )
```

profile of v0, /device:TPU:0, one launch (start us, length us, event | category | flops | bytes accessed | tf_op | source)
XLA Modules:
  0.0 422.3 jit_solution(10649243347003860131)
XLA Ops:
  7.2 0.7 all-gather.4.cloned.1.call-update
  7.9 0.7 convert_reduce_fusion
  8.6 0.6 reduce-window.6
  9.4 0.7 convert_element_type.92
  10.1 0.7 fusion.51
  10.9 0.2 select_reduce_fusion
  11.2 0.6 copy.152
  11.8 7.3 %all-to-all-start.2 = ((bf16[96,8,1]{0,2,1:T(2,128)(2,1)}), bf16[96,8,1]{0,2,1:T(2,128)(2,1)S(1)}, u32[]{:S(2)}, u32[]{:S(2)}) async-start(bf16[96,8,1]{0,2,1:T(2,128)(2,1)} %copy.152), calls=%async_computation.2 | async-start | bytes 8192 | tf_op jit(solution)/shard_map/all_to_all | solution.py:61
  19.1 4.2 %copy.139 = bf16[256,4096]{0,1:T(8,128)(2,1)} copy(bf16[256,4096]{1,0:T(8,128)(2,1)} %param.14) | data formatting | bytes 4194304 | tf_op args[0]
  23.4 2.2 all-to-all-done.2
  25.5 3.8 all-to-all-start
  29.4 0.7 all-gather.6.cloned.1.call-update
  30.2 3.4 fusion.12
  33.6 6.1 %copy.155 = bf16[96,8,4096]{2,0,1:T(8,128)(2,1)} copy(bf16[96,8,4096]{2,1,0:T(8,128)(2,1)S(1)} %fusion.12) | data formatting | bytes 12582912 | tf_op jit(solution)/shard_map/all_to_all | solution.py:60
  39.7 37.3 %all-to-all-done = bf16[256,8,512]{0,2,1:T(8,128)(2,1)S(1)} async-done(((bf16[256,8,512]{0,2,1:T(8,128)(2,1)}), bf16[256,8,512]{0,2,1:T(8,128)(2,1)S(1)}, u32[]{:S(2)}, u32[]{:S(2)}) %all-to-all-start) | async-done | bytes 2097184 | tf_op jit(solution)/shard_map/all_to_all | solution.py:58
  77.0 4.8 %all-to-all-start.3 = ((bf16[96,8,4096]{2,0,1:T(8,128)(2,1)}), bf16[96,8,4096]{2,0,1:T(8,128)(2,1)}, u32[]{:S(2)}, u32[]{:S(2)}) async-start(bf16[96,8,4096]{2,0,1:T(8,128)(2,1)} %copy.155), calls=%async_computation.3 | async-start | bytes 12582912 | tf_op jit(solution)/shard_map/all_to_all | solution.py:60
  81.8 0.7 all-gather.8.cloned.1.call-update
  82.5 4.2 copy.145
  86.7 132.3 %all-to-all-done.3 = bf16[96,8,4096]{2,0,1:T(8,128)(2,1)} async-done(((bf16[96,8,4096]{2,0,1:T(8,128)(2,1)}), bf16[96,8,4096]{2,0,1:T(8,128)(2,1)}, u32[]{:S(2)}, u32[]{:S(2)}) %all-to-all-start.3) | async-done | bytes 6291488 | tf_op jit(solution)/shard_map/all_to_all | solution.py:60
  219.0 4.4 %all-to-all-start.1 = ((bf16[256,8,512]{0,2,1:T(8,128)(2,1)}), bf16[256,8,512]{0,2,1:T(8,128)(2,1)}, u32[]{:S(2)}, u32[]{:S(2)}) async-start(bf16[256,8,512]{0,2,1:T(8,128)(2,1)} %bitcast.156), calls=%async_computation.1 | async-start | bytes 4194304 | tf_op jit(solution)/shard_map/all_to_all | solution.py:59
  223.4 0.2 reduce-scatter.2.cloned.1.call-start
  223.7 1.5 copy.153
  225.1 1.6 copy.154
  226.8 10.1 %convolution_convert_fusion.1 = bf16[768,4096]{1,0:T(8,128)(2,1)} fusion(bf16[768,4096]{1,0:T(8,128)(2,1)} %bitcast.24, bf16[1,768,768]{1,2,0:T(8,128)(2,1)S(1)} %copy.154, bf16[1,768,768]{1,2,0:T(8,128)(2,1)} %copy.153, f32[768]{0:T(1024)S(1)} %reshape.131), kind=kOutput, calls=%fused_computation.19 | convolution fusion | flops 4840292352 | bytes 14945280 | tf_op jit(solution)/shard_map/dot_general | solution.py:83
  236.9 0.7 copy-done
  237.5 0.6 sort.19
  238.3 0.9 gather_fusion
  239.9 2.5 copy.140
  242.4 2.9 reshape.124
  245.3 25.8 %all-to-all-done.1 = bf16[256,8,512]{0,2,1:T(8,128)(2,1)} async-done(((bf16[256,8,512]{0,2,1:T(8,128)(2,1)}), bf16[256,8,512]{0,2,1:T(8,128)(2,1)}, u32[]{:S(2)}, u32[]{:S(2)}) %all-to-all-start.1) | async-done | bytes 2097184 | tf_op jit(solution)/shard_map/all_to_all | solution.py:59
  271.1 4.2 copy.146
  275.3 4.1 reshape.127
  279.4 7.8 %gather_fusion.1 = bf16[64,128,512]{2,1,0:T(8,128)(2,1)} fusion(bf16[32,128,512]{2,1,0:T(8,128)(2,1)} %bitcast.153, s32[1024]{0:T(1024)S(1)} %pad_clamp_fusion), kind=kCustom, calls=%fused_computation.1.clone | custom fusion | bytes 16777472 | tf_op jit(solution)/shard_map/jit(_take)/gather | solution.py:17
  287.3 13.7 %copy.137 = bf16[16,4,128,512]{2,1,3,0:T(4,128)(2,1)} copy(bf16[16,4,128,512]{3,2,1,0:T(8,128)(2,1)} %bitcast.152) | data formatting | bytes 16777216 | tf_op jit(solution)/shard_map/jit(_take)/gather | solution.py:17
  300.9 8.5 %broadcast_select_fusion.1 = bf16[16,4,128,512]{2,1,3,0:T(4,128)(2,1)} fusion(bf16[16,4,128,512]{2,1,3,0:T(4,128)(2,1)} %copy.137, pred[16,4]{1,0:T(8,128)(4,1)S(1)} %copy.135), kind=kLoop, calls=%fused_computation.16 | loop fusion | flops 4194304 | bytes 16777280 | tf_op jit(solution)/shard_map/jit(_take)/select_n | solution.py:17
  309.4 13.1 %reshape.123 = bf16[16,512,4,128]{1,3,2,0:T(8,128)(2,1)} reshape(bf16[16,4,128,512]{2,1,3,0:T(4,128)(2,1)} %broadcast_select_fusion.1) | data formatting | bytes 16777216 | tf_op jit(solution)/shard_map/reshape | solution.py:19
  322.5 7.7 %gather_fusion.2 = bf16[64,128,512]{2,1,0:T(8,128)(2,1)} fusion(bf16[32,128,512]{2,1,0:T(8,128)(2,1)} %bitcast.154, s32[1024]{0:T(1024)S(1)} %pad_clamp_fusion), kind=kCustom, calls=%fused_computation.2.clone | custom fusion | bytes 16777472 | tf_op jit(solution)/shard_map/jit(_take)/gather | solution.py:17
  330.2 7.5 %broadcast_select_fusion = bf16[16,4,128,512]{3,2,1,0:T(8,128)(2,1)} fusion(bf16[16,4,128,512]{3,2,1,0:T(8,128)(2,1)} %bitcast.151, pred[16,4]{1,0:T(8,128)(4,1)S(1)} %copy.135), kind=kLoop, calls=%fused_computation.15 | loop fusion | flops 4194304 | bytes 16777280 | tf_op jit(solution)/shard_map/jit(_take)/select_n | solution.py:17
  337.7 12.5 %reshape.126 = bf16[16,512,4,128]{3,2,1,0:T(4,128)(2,1)} reshape(bf16[16,4,128,512]{3,2,1,0:T(8,128)(2,1)} %broadcast_select_fusion) | data formatting | bytes 16777216 | tf_op jit(solution)/shard_map/reshape | solution.py:19
  350.2 10.8 %bitcast_reduce_fusion = (f32[16,4,128]{2,1,0:T(4,128)S(1)}, f32[16,4,512,128]{3,2,1,0:T(8,128)}) fusion(pred[16,512]{1,0:T(8,128)(4,1)S(1)} %bitcast.160, bf16[16,512,4,128]{1,3,2,0:T(8,128)(2,1)} %reshape.123, bf16[16,128,4,128]{1,0,3,2:T(8,128)(2,1)S(1)} %reshape.124), kind=kOutput, calls=%fused_computation.9 | convolution fusion | flops 1086316544 | bytes 27303936 | tf_op jit(solution)/shard_map/bqhd,bkhd->bhqk/dot_general | solution.py:135
  361.1 16.7 %fusion.5 = (f32[16,4,128]{2,1,0:T(4,128)S(1)}, f32[16,4,128]{2,1,0:T(4,128)S(1)}, f32[16,4,512,128]{3,2,1,0:T(8,128)}) fusion(f32[16,4,512,128]{3,2,1,0:T(8,128)} %get-tuple-element.48, f32[16,4,128]{2,1,0:T(4,128)S(1)} %broadcast_maximum_fusion, pred[16,512]{1,0:T(8,128)(4,1)S(1)} %bitcast.161, bf16[16,128,4,128]{1,0,3,2:T(8,128)(2,1)S(1)} %copy-done.2, ...), kind=kOutput, calls=%fused_computation.12 | convolution fusion | flops 1103085568 | bytes 44146688 | tf_op jit(solution)/shard_map/bqhd,bkhd->bhqk/dot_general | solution.py:141
  377.8 17.6 %fusion.32 = bf16[16,128,4,128]{1,3,2,0:T(8,128)(2,1)} fusion(bf16[16,512,4,128]{1,3,2,0:T(8,128)(2,1)} %reshape.123, f32[16,4,512,128]{3,2,1,0:T(8,128)} %get-tuple-element.49, f32[16,4,512,128]{3,2,1,0:T(8,128)} %get-tuple-element.48, f32[16,4,128]{2,1,0:T(4,128)S(1)} %div.30, f32[16,4,128]{2,1,0:T(4,128)S(1)} %get-tuple-element.39, ...), kind=kOutput, calls=%fused_computation.49 | convolution fusion | flops 1105199104 | bytes 44146688 | tf_op jit(solution)/shard_map/bhqk,bkhd->bqhd/dot_general | solution.py:145
  395.5 3.2 copy.161
  398.6 1.7 copy.179
  400.3 11.1 %fusion.22 = (f32[768]{0:T(1024)S(1)}, bf16[1,768,768]{1,2,0:T(8,128)(2,1)}, bf16[1,768,768]{1,2,0:T(8,128)(2,1)S(1)}) fusion(bf16[1,768,768]{1,2,0:T(8,128)(2,1)} %copy-done.5, bf16[1,768,768]{1,2,0:T(8,128)(2,1)S(1)} %copy-done.4, f32[768]{0:T(1024)S(1)} %reshape.131, bf16[768,4096]{1,0:T(8,128)(2,1)} %bitcast.24, ...), kind=kOutput, calls=%fused_computation.38 | convolution fusion | flops 4843043840 | bytes 17307648 | tf_op jit(solution)/shard_map/dot_general | solution.py:64
  411.4 2.4 copy.157
  413.8 1.4 copy.158
  415.2 0.6 broadcast_in_dim.80
  (46 shorter events, 1.6 us)
Async XLA Ops:
  7.2 272.3 %all-gather.4.cloned.1.call-start = ((), (), s32[]{:S(2)}) async-start(), calls=%async_computation.5 | async-start | bytes 5242880 | tf_op jit(solution)/shard_map/all_gather | solution.py:129
  11.8 13.7 %all-to-all-start.2 = ((bf16[96,8,1]{0,2,1:T(2,128)(2,1)}), bf16[96,8,1]{0,2,1:T(2,128)(2,1)S(1)}, u32[]{:S(2)}, u32[]{:S(2)}) async-start(bf16[96,8,1]{0,2,1:T(2,128)(2,1)} %copy.152), calls=%async_computation.2 | async-start | bytes 8192 | tf_op jit(solution)/shard_map/all_to_all | solution.py:61
  25.5 51.5 %all-to-all-start = ((bf16[256,8,512]{0,2,1:T(8,128)(2,1)}), bf16[256,8,512]{0,2,1:T(8,128)(2,1)S(1)}, u32[]{:S(2)}, u32[]{:S(2)}) async-start(bf16[256,8,512]{0,2,1:T(8,128)(2,1)} %bitcast.157), calls=%async_computation | async-start | bytes 4194304 | tf_op jit(solution)/shard_map/all_to_all | solution.py:58
  29.3 293.2 %all-gather.6.cloned.1.call-start = ((), (), s32[]{:S(2)}) async-start(), calls=%async_computation.6 | async-start | bytes 5242880 | tf_op jit(solution)/shard_map/all_gather | solution.py:130
  77.0 142.0 %all-to-all-start.3 = ((bf16[96,8,4096]{2,0,1:T(8,128)(2,1)}), bf16[96,8,4096]{2,0,1:T(8,128)(2,1)}, u32[]{:S(2)}, u32[]{:S(2)}) async-start(bf16[96,8,4096]{2,0,1:T(8,128)(2,1)} %copy.155), calls=%async_computation.3 | async-start | bytes 12582912 | tf_op jit(solution)/shard_map/all_to_all | solution.py:60
  81.8 318.5 %all-gather.8.cloned.1.call-start = ((), (), s32[]{:S(2)}) async-start(), calls=%async_computation.8 | async-start | bytes 7864320 | tf_op jit(solution)/shard_map/all_gather | solution.py:66
  82.5 141.1 %copy-start.3 = (bf16[1,768,768]{2,1,0:T(8,128)(2,1)S(1)}, bf16[1,768,768]{2,1,0:T(8,128)(2,1)}, u32[]{:S(2)}) copy-start(bf16[1,768,768]{2,1,0:T(8,128)(2,1)} %param.21) | copy-start | bytes 3538948
  219.0 52.1 %all-to-all-start.1 = ((bf16[256,8,512]{0,2,1:T(8,128)(2,1)}), bf16[256,8,512]{0,2,1:T(8,128)(2,1)}, u32[]{:S(2)}, u32[]{:S(2)}) async-start(bf16[256,8,512]{0,2,1:T(8,128)(2,1)} %bitcast.156), calls=%async_computation.1 | async-start | bytes 4194304 | tf_op jit(solution)/shard_map/all_to_all | solution.py:59
  223.4 192.4 %reduce-scatter.2.cloned.1.call-start = ((), (), s32[]{:S(2)}) async-start(), calls=%async_computation.7 | async-start | bytes 7864320 | tf_op jit(solution)/shard_map/reduce_scatter | solution.py:82
  226.7 10.2 %copy-start.5 = (bf16[1,768,768]{1,2,0:T(8,128)(2,1)}, bf16[1,768,768]{1,2,0:T(8,128)(2,1)S(1)}, u32[]{:S(2)}) copy-start(bf16[1,768,768]{1,2,0:T(8,128)(2,1)S(1)} %copy.154) | copy-start | bytes 3538948
  236.8 0.7 copy-start
  350.2 10.8 %copy-start.1 = (bf16[16,512,4,128]{3,2,1,0:T(4,128)(2,1)S(1)}, bf16[16,512,4,128]{3,2,1,0:T(4,128)(2,1)}, u32[]{:S(2)}) copy-start(bf16[16,512,4,128]{3,2,1,0:T(4,128)(2,1)} %reshape.126) | copy-start | bytes 25165828
  350.2 10.8 %copy-start.2 = (bf16[16,128,4,128]{1,0,3,2:T(8,128)(2,1)S(1)}, bf16[16,128,4,128]{1,0,3,2:T(8,128)(2,1)}, u32[]{:S(2)}) copy-start(bf16[16,128,4,128]{1,0,3,2:T(8,128)(2,1)} %reshape.127) | copy-start | bytes 6291460
  395.5 4.8 %copy-start.4 = (bf16[1,768,768]{1,2,0:T(8,128)(2,1)S(1)}, bf16[1,768,768]{1,2,0:T(8,128)(2,1)}, u32[]{:S(2)}) copy-start(bf16[1,768,768]{1,2,0:T(8,128)(2,1)} %copy.153) | copy-start | bytes 3538948
Sparse Core Ops, SparseCore 0:
  9.5 37.1 all-gather.3
  48.3 34.4 all-gather.5
  84.4 47.4 all-gather.7
  237.0 59.9 reduce-scatter.1
where the time goes:
time: 424 us; the launch traced here: 422 us
  waiting for transfers between devices  200 us (47%)
  local copies, waits for them, and re-layouts  98.8 us (23%)
  matrix products  69.7 us (16%)
  starting transfers between devices  20.6 us (5%)
  other arithmetic  19.7 us (5%)
  between operations  13.9 us (3%)
    all_to_all x1, waiting for transfers between devices, per_device(): lax.all_to_all(slot_rows, 'expert', split_axis=1, concat_axis=0, tiled=True)  132 us
    all_to_all x1, waiting for transfers between devices, per_device(): lax.all_to_all(queries, 'expert', split_axis=1, concat_axis=0, tiled=True)  37.3 us
    gather x3, local copies, waits for them, and re-layouts, pick_blocks(): jnp.take(source_rows.reshape(block_count, QBLK, source_rows.shape[1]), cl...  29.2 us
    all_to_all x1, waiting for transfers between devices, per_device(): lax.all_to_all(out_grad, 'expert', split_axis=1, concat_axis=0, tiled=True)  25.8 us
    reshape x2, local copies, waits for them, and re-layouts, pick_blocks(): blocks.reshape(batch_size, chosen.shape[1] * QBLK, source_rows.shape[1] /...  25.6 us
    unnamed x21, local copies, waits for them, and re-layouts  20.8 us
    dot_general x1, matrix products, per_device(): jnp.einsum('bhqk,bkhd->bqhd', grad_scores, picked_keys, preferred_element...  17.6 us
    dot_general x1, matrix products, per_device(): jnp.einsum('bqhd,bkhd->bhqk', grad_blocks, picked_values, preferred_eleme...  16.7 us
  transfers between devices with their start and end apart: 8, of which 4 were waited for; matrix products, arithmetic and copies ran while one was open for 44% of the time, Pallas kernels for 0%

commit v1 on v0

v1 whole, which is shorter than its diff:
```python
import functools

import jax
import jax.numpy as jnp
from jax import lax
from jax.experimental import pallas as pl
from jax.experimental.pallas import tpu as pltpu
from jax.sharding import PartitionSpec as P

HD = 128
QBLK = 128
DOT_NT = (((1,), (1,)), ((), ()))


def attend_kernel(idx_ref, half_ref, q_ref, near_ref, far_ref, k_ref, v_ref, o_ref):
    b = pl.program_id(0)
    side = b // (pl.num_programs(0) // 2)
    is_near = side == half_ref[0]
    ksel = idx_ref.shape[1]
    scale = 1.0 / HD**0.5
    starts = [pl.multiple_of(idx_ref[b, j] * QBLK, QBLK) for j in range(ksel)]
    for head in range(q_ref.shape[1] // HD):
        cols = slice(head * HD, (head + 1) * HD)
        q = q_ref[:, cols]
        g = jnp.where(is_near, near_ref[:, cols], far_ref[:, cols])
        k = jnp.concatenate([k_ref[pl.ds(s, QBLK), cols] for s in starts], axis=0)
        v = jnp.concatenate([v_ref[pl.ds(s, QBLK), cols] for s in starts], axis=0)
        scores = lax.dot_general(q, k, DOT_NT, preferred_element_type=jnp.float32) * scale
        grad_probs = lax.dot_general(g, v, DOT_NT, preferred_element_type=jnp.float32)
        weights = jnp.exp(scores - jnp.max(scores, axis=-1, keepdims=True))
        inverse = 1.0 / jnp.sum(weights, axis=-1, keepdims=True)
        delta = jnp.sum(weights * grad_probs, axis=-1, keepdims=True) * inverse
        grad_scores = (weights * inverse * (grad_probs - delta)).astype(jnp.bfloat16)
        out = jnp.dot(grad_scores, k, preferred_element_type=jnp.float32) * scale
        o_ref[:, cols] = out.astype(o_ref.dtype)


def attend(block_index, my_half, queries, near, far, keys, values):
    rows, width = queries.shape
    blocks = rows // QBLK
    per_side = blocks // 2

    def side_map(b, idx, half, want_near):
        mine = (b // per_side) == half[0]
        use = mine if want_near else jnp.logical_not(mine)
        return (jnp.where(use, b % per_side, 0), 0)

    whole = pl.BlockSpec(keys.shape, lambda b, *_: (0, 0), pipeline_mode=pl.Buffered(1))
    return pl.pallas_call(
        attend_kernel,
        out_shape=jax.ShapeDtypeStruct((rows, width), jnp.bfloat16),
        grid_spec=pltpu.PrefetchScalarGridSpec(
            num_scalar_prefetch=2,
            grid=(blocks,),
            in_specs=[
                pl.BlockSpec((QBLK, width), lambda b, *_: (b, 0)),
                pl.BlockSpec((QBLK, width), functools.partial(side_map, want_near=True)),
                pl.BlockSpec((QBLK, width), functools.partial(side_map, want_near=False)),
                whole,
                whole,
            ],
            out_specs=pl.BlockSpec((QBLK, width), lambda b, *_: (b, 0)),
        ),
        compiler_params=pltpu.CompilerParams(vmem_limit_bytes=40 * 2**20),
        cost_estimate=pl.CostEstimate(
            flops=6 * rows * width * block_index.shape[1] * QBLK,
            bytes_accessed=2 * (2 * keys.size + 3 * queries.size),
            transcendentals=rows * width // HD * block_index.shape[1] * QBLK,
        ),
    )(block_index, my_half, queries, near, far, keys, values)


def down_kernel(wt_ref, near_ref, far_ref, o_ref):
    cut = near_ref.shape[0]
    total = jnp.dot(wt_ref[:, :cut], near_ref[...], preferred_element_type=jnp.float32)
    total += jnp.dot(wt_ref[:, cut:], far_ref[...], preferred_element_type=jnp.float32)
    o_ref[...] = total.astype(o_ref.dtype)


def down_terms(weighted_t, near, far):
    ff, slots = weighted_t.shape
    cut, width = near.shape
    tile = min(1024, width)
    return pl.pallas_call(
        down_kernel,
        out_shape=jax.ShapeDtypeStruct((ff, width), jnp.bfloat16),
        grid=(width // tile,),
        in_specs=[
            pl.BlockSpec((ff, slots), lambda i: (0, 0)),
            pl.BlockSpec((cut, tile), lambda i: (0, i)),
            pl.BlockSpec((slots - cut, tile), lambda i: (0, i)),
        ],
        out_specs=pl.BlockSpec((ff, tile), lambda i: (0, i)),
        compiler_params=pltpu.CompilerParams(vmem_limit_bytes=40 * 2**20),
        cost_estimate=pl.CostEstimate(
            flops=2 * ff * slots * width,
            bytes_accessed=2 * (ff * slots + slots * width + ff * width),
            transcendentals=0,
        ),
    )(weighted_t, near, far)


def slot_kernel(
    half_ref, near_ref, far_ref, w_ref, gate_ref, up_ref, sw_ref, gg_ref, ug_ref, cg_ref, acc
):
    step = pl.program_id(0)
    cut = near_ref.shape[0]

    @pl.when(step == 0)
    def _():
        acc[...] = jnp.zeros_like(acc)

    w = w_ref[...]
    acc[:cut, :] += lax.dot_general(near_ref[...], w, DOT_NT, preferred_element_type=jnp.float32)
    acc[cut:, :] += lax.dot_general(far_ref[...], w, DOT_NT, preferred_element_type=jnp.float32)

    @pl.when(step == pl.num_programs(0) - 1)
    def _():
        for part in range(2):
            side = half_ref[0] if part == 0 else 1 - half_ref[0]
            rows = pl.ds(pl.multiple_of(side * cut, cut), cut)
            back = acc[part * cut : (part + 1) * cut, :]
            gate = gate_ref[rows, :].astype(jnp.float32)
            up = up_ref[rows, :].astype(jnp.float32)
            sig = jax.nn.sigmoid(gate)
            silu = gate * sig
            cg_ref[rows, :] = jnp.sum(silu * up * back, axis=-1, keepdims=True)
            hidden_grad = sw_ref[rows, :] * back
            gg_ref[rows, :] = (hidden_grad * up * sig * (1.0 + gate * (1.0 - sig))).astype(
                jnp.bfloat16
            )
            ug_ref[rows, :] = (hidden_grad * silu).astype(jnp.bfloat16)


def slot_grads(my_half, near, far, weights, gate, up, slot_weight):
    cut, width = near.shape
    slots, ff = gate.shape
    tile = min(512, width)

    def full(shape):
        return pl.BlockSpec(shape, lambda i, *_: (0, 0), pipeline_mode=pl.Buffered(1))

    return pl.pallas_call(
        slot_kernel,
        out_shape=(
            jax.ShapeDtypeStruct((slots, ff), jnp.bfloat16),
            jax.ShapeDtypeStruct((slots, ff), jnp.bfloat16),
            jax.ShapeDtypeStruct((slots, 1), jnp.float32),
        ),
        grid_spec=pltpu.PrefetchScalarGridSpec(
            num_scalar_prefetch=1,
            grid=(width // tile,),
            in_specs=[
                pl.BlockSpec((cut, tile), lambda i, *_: (0, i)),
                pl.BlockSpec((slots - cut, tile), lambda i, *_: (0, i)),
                pl.BlockSpec((ff, tile), lambda i, *_: (0, i)),
                full((slots, ff)),
                full((slots, ff)),
                full((slots, 1)),
            ],
            out_specs=(
                pl.BlockSpec((slots, ff), lambda i, *_: (0, 0)),
                pl.BlockSpec((slots, ff), lambda i, *_: (0, 0)),
                pl.BlockSpec((slots, 1), lambda i, *_: (0, 0)),
            ),
            scratch_shapes=[pltpu.VMEM((slots, ff), jnp.float32)],
        ),
        compiler_params=pltpu.CompilerParams(vmem_limit_bytes=40 * 2**20),
        cost_estimate=pl.CostEstimate(
            flops=2 * ff * slots * width,
            bytes_accessed=2 * (4 * ff * slots + slots * width + ff * width),
            transcendentals=slots * ff,
        ),
    )(my_half, near, far, weights, gate, up, slot_weight)


def before_count(hits):
    tokens = hits.shape[-1]
    earlier = jnp.triu(jnp.ones((tokens, tokens), jnp.bfloat16), 1)
    return lax.dot_general(
        hits.astype(jnp.bfloat16), earlier, (((1,), (0,)), ((), ())),
        preferred_element_type=jnp.float32,
    )


def placing_of(routes_t, experts, capacity):
    hits = jnp.any(routes_t[None, :, :] == experts[:, None, None], axis=1)
    before = before_count(hits)
    ranks = jnp.arange(capacity, dtype=jnp.float32)[None, :, None]
    placing = (before[:, None, :] == ranks) & hits[:, None, :]
    return placing.astype(jnp.bfloat16).reshape(-1, routes_t.shape[1])


def per_device(
    queries, out_grad, mem_keys, mem_values, block_index, routes, combine, gate_pre, up_pre, w_down
):
    experts = lax.axis_size("expert")
    half = experts // 2
    me = lax.axis_index("expert")
    my_half = me // half
    tokens, width = out_grad.shape
    slots, ff = gate_pre.shape[1:]
    capacity = slots // experts
    head_cols = width // experts
    groups = [list(range(half)), list(range(half, experts))]
    partner = [(i, (i + half) % experts) for i in range(experts)]

    routes_t = routes.T
    packed = jnp.concatenate([routes_t.astype(jnp.float32), combine.T.astype(jnp.float32)], axis=0)
    topk = routes_t.shape[0]

    far_grad = lax.ppermute(out_grad, "expert", partner)
    far_routes = lax.ppermute(routes_t, "expert", partner)
    packed_all = lax.all_gather(packed, "expert", axis=0, tiled=False)

    here = my_half * half + jnp.arange(half, dtype=jnp.int32)

    def exchange(rows, rows_routes):
        placing = placing_of(rows_routes, here, capacity)
        picked = jnp.dot(placing, rows, preferred_element_type=jnp.float32).astype(jnp.bfloat16)
        slot_rows = lax.all_to_all(
            picked.reshape(half, capacity, width), "expert", split_axis=0, concat_axis=0,
            axis_index_groups=groups, tiled=True,
        ).reshape(half * capacity, width)
        columns = lax.dynamic_slice_in_dim(rows, my_half * half * head_cols, half * head_cols, 1)
        columns = columns.reshape(tokens, half, head_cols).transpose(1, 0, 2)
        columns = lax.all_to_all(
            columns, "expert", split_axis=0, concat_axis=0, axis_index_groups=groups, tiled=True
        ).reshape(half * tokens, head_cols)
        return slot_rows, columns

    near_rows, near_cols = exchange(out_grad, routes_t)
    far_rows, far_cols = exchange(far_grad, far_routes)
    head_queries = lax.all_to_all(
        queries.reshape(tokens, experts, head_cols).transpose(1, 0, 2),
        "expert", split_axis=0, concat_axis=0, tiled=True,
    ).reshape(experts * tokens, head_cols)

    keys = lax.all_gather(mem_keys, "mem", axis=0, tiled=True)
    values = lax.all_gather(mem_values, "mem", axis=0, tiled=True)
    weights = lax.all_gather(w_down, "mem", axis=1, tiled=True)[0]

    named = packed_all[:, :topk, :] == me.astype(jnp.float32)
    hits = jnp.any(named, axis=1)
    token_weight = jnp.sum(jnp.where(named, packed_all[:, topk:, :], 0.0), axis=1)
    ranks = jnp.arange(capacity, dtype=jnp.float32)[None, :, None]
    filled = (before_count(hits)[:, None, :] == ranks) & hits[:, None, :]
    slot_weight = jnp.sum(jnp.where(filled, token_weight[:, None, :], 0.0), axis=2)
    slot_weight = slot_weight.reshape(slots, 1)

    gate_val = gate_pre[0].astype(jnp.float32)
    up_val = up_pre[0].astype(jnp.float32)
    weighted = (slot_weight * (gate_val * jax.nn.sigmoid(gate_val) * up_val)).astype(jnp.bfloat16)
    swapped = jnp.roll(weighted, half * capacity, axis=0)
    weighted_t = jnp.where(my_half == 0, weighted, swapped).T

    w_down_grad = lax.psum_scatter(
        down_terms(weighted_t, near_rows, far_rows), "mem", scatter_dimension=0, tiled=True
    )[None]
    side = my_half.astype(jnp.int32).reshape(1)
    query_grad = attend(block_index, side, head_queries, near_cols, far_cols, keys, values)
    gate_grad, up_grad, combine_grad = slot_grads(
        side, near_rows, far_rows, weights, gate_pre[0], up_pre[0], slot_weight
    )
    return (
        query_grad, w_down_grad, gate_grad[None], up_grad[None], combine_grad.reshape(1, slots)
    )


def solution(mesh):
    in_specs = (
        P(("mem", "expert"), None),
        P(("mem", "expert"), None),
        P("mem", "expert"),
        P("mem", "expert"),
        P("mem", None),
        P(("mem", "expert"), None),
        P(("mem", "expert"), None),
        P("expert", "mem", None),
        P("expert", "mem", None),
        P("expert", "mem", None),
    )
    out_specs = (
        P("mem", "expert"),
        P("expert", "mem", None),
        P("expert", "mem", None),
        P("expert", "mem", None),
        P("expert", "mem"),
    )
    return jax.shard_map(
        per_device, mesh=mesh, in_specs=in_specs, out_specs=out_specs, check_vma=False
    )
```

time: 424 us -> 345 us (0.81)
  local copies, waits for them, and re-layouts: 98.8 us -> 34.2 us
  matrix products: 69.7 us -> 5.83 us
  blocking collectives: 0 us -> 60.6 us
  waiting for transfers between devices: 200 us -> 148 us
  Pallas kernels: 0 us -> 49.1 us
  other arithmetic: 19.7 us -> 4.52 us
  starting transfers between devices: 20.6 us -> 26.7 us
    all_to_all x4 -> x5, waiting for transfers between devices: 198 us -> 55 us  [the longest x2 31.5 us: exchange(): lax.all_to_all(columns, 'expert', split_axis=0, concat_axis=0, axis_index...]
    ppermute x0 -> x2, waiting for transfers between devices: none -> 91.2 us  [the longest x1 89.7 us: per_device(): far_grad = lax.ppermute(out_grad, 'expert', partner)]
    dot_general x6 -> x5, matrix products: 69.7 us -> 5.83 us  [the longest x2 5.4 us: exchange(): jnp.dot(placing, rows, preferred_element_type=jnp.float32)]
    all_gather x0 -> x1, blocking collectives: none -> 60.6 us  [per_device(): packed_all = lax.all_gather(packed, 'expert', axis=0, tiled=False)]
    pallas_call x0 -> x3, Pallas kernels: none -> 49.1 us  [the longest x1 27.5 us: attend(): pl.pallas_call(attend_kernel, out_shape=jax.ShapeDtypeStruct((rows, width...]
    gather x8 -> x0, local copies, waits for them, and re-layouts: 30.4 us -> none  [the longest x3 29.2 us: pick_blocks(): jnp.take(source_rows.reshape(block_count, QBLK, source_rows.shape[1]), cl...]
    reshape x4 -> x3, local copies, waits for them, and re-layouts: 32.7 us -> 3.96 us  [the longest x1 3.11 us: per_device(): queries.reshape(tokens, experts, head_cols).transpose(1, 0, 2)]
    select_n x2 -> x0, other arithmetic: 16 us -> none  [pick_blocks(): jnp.take(source_rows.reshape(block_count, QBLK, source_rows.shape[1]), cl...]
  transfers between devices with their start and end apart: 8 -> 11, of which waited for: 4 -> 5; matrix products, arithmetic and copies ran while one was open for 44% -> 8% of each run, Pallas kernels for 0% -> 14%
where the time goes in v1:
time: 345 us; the launch traced here: 343 us
  waiting for transfers between devices  148 us (43%)
  blocking collectives  60.6 us (18%)
  Pallas kernels  49.1 us (14%)
  local copies, waits for them, and re-layouts  34.2 us (10%)
  starting transfers between devices  26.7 us (8%)
  between operations  14 us (4%)
  matrix products  5.83 us (2%)
  other arithmetic  4.52 us (1%)
    ppermute x1, waiting for transfers between devices, per_device(): far_grad = lax.ppermute(out_grad, 'expert', partner)  89.7 us
    all_gather x1, blocking collectives, per_device(): packed_all = lax.all_gather(packed, 'expert', axis=0, tiled=False)  60.6 us
    all_to_all x2, waiting for transfers between devices, exchange(): lax.all_to_all(columns, 'expert', split_axis=0, concat_axis=0, axis_index...  31.5 us
    pallas_call x1, Pallas kernels, attend(): pl.pallas_call(attend_kernel, out_shape=jax.ShapeDtypeStruct((rows, width...  27.5 us
    all_to_all x1, waiting for transfers between devices, per_device(): lax.all_to_all(queries.reshape(tokens, experts, head_cols).transpose(1, 0...  23.5 us
    unnamed x36, local copies, waits for them, and re-layouts  20.4 us
    pallas_call x1, Pallas kernels, slot_grads(): pl.pallas_call(slot_kernel, out_shape=(jax.ShapeDtypeStruct((slots, ff),...  12.7 us
    pallas_call x1, Pallas kernels, down_terms(): pl.pallas_call(down_kernel, out_shape=jax.ShapeDtypeStruct((ff, width), j...  8.92 us
  transfers between devices with their start and end apart: 11, of which 5 were waited for; matrix products, arithmetic and copies ran while one was open for 8% of the time, Pallas kernels for 14%

profile of v1, /device:TPU:0, one launch (start us, length us, event | category | flops | bytes accessed | tf_op | source)
XLA Modules:
  0.0 343.4 jit_solution(3165881593855388659)
XLA Ops:
  7.2 0.7 all-gather.6.cloned.1.call-update
  8.0 0.7 all-gather.8.cloned.1.call-update
  8.7 4.1 %collective-permute-start.1 = (s32[2,256]{1,0:T(2,128)S(1)}, s32[2,256]{1,0:T(2,128)S(1)}, u32[]{:S(2)}, u32[]{:S(2)}) collective-permute-start(s32[2,256]{1,0:T(2,128)S(1)} %bitcast.67), channel_id=1, source_target_pairs={{0,4},{1,5},{2,6},{3,7},{4,0},{5,1},{6,2},{7,3},{8,12},{9,13},{10,... | collective-permute-start | bytes 6152 | tf_op jit(solution)/shard_map/ppermute | solution.py:213
  12.9 1.5 collective-permute-done.1
  14.5 0.2 fusion.11
  14.6 0.1 fusion.13
  14.8 0.2 fusion.9
  15.0 2.7 convolution_convert_fusion.1
  17.7 4.1 %all-to-all-start.3 = ((bf16[4,96,4096]{2,1,0:T(8,128)(2,1)}), bf16[4,96,4096]{2,1,0:T(8,128)(2,1)S(1)}, u32[]{:S(2)}, u32[]{:S(2)}) async-start(bf16[4,96,4096]{2,1,0:T(8,128)(2,1)} %bitcast.64), calls=%async_computation.3 | async-start | bytes 6291456 | tf_op jit(solution)/shard_map/all_to_all | solution.py:221
  21.8 0.7 all-gather.10.cloned.1.call-update
  22.5 4.1 %copy.35 = bf16[256,4096]{0,1:T(8,128)(2,1)} copy(bf16[256,4096]{1,0:T(8,128)(2,1)} %param.11) | data formatting | bytes 4194304 | tf_op args[1]
  26.6 2.6 collective-permute-start
  29.2 89.7 %collective-permute-done = bf16[256,4096]{0,1:T(8,128)(2,1)S(1)} collective-permute-done((bf16[256,4096]{0,1:T(8,128)(2,1)}, bf16[256,4096]{0,1:T(8,128)(2,1)S(1)}, u32[]{:S(2)}, u32[]{:S(2)}) %collective-permute-start) | collective-permute-done | bytes 2097184 | tf_op jit(solution)/shard_map/ppermute | solution.py:212
  119.0 1.4 copy-done.10
  120.3 2.7 convolution_convert_fusion
  123.0 4.8 %all-to-all-start.4 = ((bf16[4,96,4096]{2,1,0:T(8,128)(2,1)}), bf16[4,96,4096]{2,1,0:T(8,128)(2,1)}, u32[]{:S(2)}, u32[]{:S(2)}) async-start(bf16[4,96,4096]{2,1,0:T(8,128)(2,1)} %bitcast.63), calls=%async_computation.4 | async-start | bytes 6291456 | tf_op jit(solution)/shard_map/all_to_all | solution.py:221
  127.9 60.6 %all-gather.1 = f32[8,4,256]{2,1,0:T(4,128)S(1)} all-gather(f32[1,4,256]{2,1,0:T(4,128)S(1)} %maximum_bitcast_fusion), channel_id=2, replica_groups=mesh['mem'=4,'expert'=8] {'expert'}, dimensions={0}, use_global_device_ids=true | all-gather | bytes 36864 | tf_op jit(solution)/shard_map/all_gather | solution.py:214
  188.6 0.1 fusion.15
  188.8 0.3 select_reduce_fusion
  189.1 2.4 fusion.5
  191.6 1.3 fusion.6
  192.9 2.4 copy.40.wt_ref
  195.3 1.3 copy-done.6
  196.6 8.9 %shard_map.138 = bf16[768,4096]{1,0:T(8,128)(2,1)S(1)} custom-call(bf16[768,768]{1,0:T(8,128)(2,1)S(1)} %copy-done.6, bf16[384,4096]{1,0:T(8,128)(2,1)S(1)} %bitcast.59, bf16[384,4096]{1,0:T(8,128)(2,1)} %bitcast.22.far_ref), custom_call_target="tpu_custom_call" | custom-call | flops 4831838208 | bytes 13762560 | tf_op jit(solution)/shard_map/pallas_call | solution.py:84
  205.5 2.6 copy-done
  208.1 2.4 constant_dynamic-slice_fusion.1
  210.6 3.5 %all-to-all-start.1 = ((bf16[4,256,512]{1,2,0:T(8,128)(2,1)}), bf16[4,256,512]{1,2,0:T(8,128)(2,1)S(1)}, u32[]{:S(2)}, u32[]{:S(2)}) async-start(bf16[4,256,512]{1,2,0:T(8,128)(2,1)} %bitcast.4), calls=%async_computation.1 | async-start | bytes 2097152 | tf_op jit(solution)/shard_map/all_to_all | solution.py:227
  214.1 1.0 constant_dynamic-slice_fusion
  215.1 12.9 %all-to-all-done.1 = bf16[4,256,512]{1,2,0:T(8,128)(2,1)S(1)} async-done(((bf16[4,256,512]{1,2,0:T(8,128)(2,1)}), bf16[4,256,512]{1,2,0:T(8,128)(2,1)S(1)}, u32[]{:S(2)}, u32[]{:S(2)}) %all-to-all-start.1) | async-done | bytes 1048608 | tf_op jit(solution)/shard_map/all_to_all | solution.py:227
  228.0 3.6 %all-to-all-start.2 = ((bf16[4,256,512]{1,2,0:T(8,128)(2,1)}), bf16[4,256,512]{1,2,0:T(8,128)(2,1)S(1)}, u32[]{:S(2)}, u32[]{:S(2)}) async-start(bf16[4,256,512]{1,2,0:T(8,128)(2,1)} %bitcast.7), calls=%async_computation.2 | async-start | bytes 2097152 | tf_op jit(solution)/shard_map/all_to_all | solution.py:227
  231.7 3.1 copy.44
  234.8 18.6 %all-to-all-done.2 = bf16[4,256,512]{1,2,0:T(8,128)(2,1)S(1)} async-done(((bf16[4,256,512]{1,2,0:T(8,128)(2,1)}), bf16[4,256,512]{1,2,0:T(8,128)(2,1)S(1)}, u32[]{:S(2)}, u32[]{:S(2)}) %all-to-all-start.2) | async-done | bytes 1048608 | tf_op jit(solution)/shard_map/all_to_all | solution.py:227
  253.4 1.0 copy-done.13
  254.4 3.8 %all-to-all-start = ((bf16[8,256,512]{2,1,0:T(8,128)(2,1)}), bf16[8,256,512]{2,1,0:T(8,128)(2,1)S(1)}, u32[]{:S(2)}, u32[]{:S(2)}) async-start(bf16[8,256,512]{2,1,0:T(8,128)(2,1)} %bitcast.65), calls=%async_computation | async-start | bytes 4194304 | tf_op jit(solution)/shard_map/all_to_all | solution.py:234
  258.2 0.3 reshape.88.sw_ref
  258.5 1.5 copy.36
  260.0 2.3 copy.38
  262.3 23.5 %all-to-all-done = bf16[8,256,512]{2,1,0:T(8,128)(2,1)S(1)} async-done(((bf16[8,256,512]{2,1,0:T(8,128)(2,1)}), bf16[8,256,512]{2,1,0:T(8,128)(2,1)S(1)}, u32[]{:S(2)}, u32[]{:S(2)}) %all-to-all-start) | async-done | bytes 2097184 | tf_op jit(solution)/shard_map/all_to_all | solution.py:234
  285.8 2.2 copy-done.1
  288.0 2.2 copy-done.2
  290.2 1.2 copy-done.3
  291.4 27.5 %shard_map.137 = bf16[2048,512]{1,0:T(8,128)(2,1)} custom-call(s32[16,4]{1,0:T(8,128)S(1)} %copy.39.idx_ref, s32[1]{0:T(128)} %bitcast.half_ref, bf16[2048,512]{1,0:T(8,128)(2,1)S(1)} %bitcast.56, bf16[1024,512]{1,0:T(8,128)(2,1)S(1)} %bitcast.57, bf16[1024,512]{1,0:T(8,128)(2,1)S(1)} %bitcast.58, bf16[4096,512]{1,0:T(8,128)(2,1)S(1)} %copy-done.1, ...), custom_call_target="tpu_custom_call" | custom-call | flops 3221225472 | bytes 14680064 | tf_op jit(solution)/shard_map/pallas_call | solution.py:49
  319.0 1.9 copy-done.5
  320.8 1.3 copy-done.7
  322.1 1.3 copy-done.8
  323.4 12.7 %shard_map.139 = (bf16[768,768]{1,0:T(8,128)(2,1)}, bf16[768,768]{1,0:T(8,128)(2,1)}, f32[768,1]{1,0:T(8,128)S(1)}) custom-call(s32[1]{0:T(128)} %bitcast.half_ref, bf16[384,4096]{1,0:T(8,128)(2,1)S(1)} %bitcast.60, bf16[384,4096]{1,0:T(8,128)(2,1)} %bitcast.22.far_ref, bf16[768,4096]{1,0:T(8,128)(2,1)} %bitcast.69, bf16[768,768]{1,0:T(8,128)(2,1)S(1)} %bitcast.62, ...), custom_call_target="tpu_custom_call" | custom-call | flops 4831838208 | bytes 17301504 | tf_op jit(solution)/shard_map/pallas_call | solution.py:143
  336.1 0.2 reduce
  336.3 0.6 reshape.83
  (47 shorter events, 0.7 us)
Async XLA Ops:
  7.2 1.5 copy-start.14
  7.2 7.8 %copy-start.9 = (bf16[256,4096]{1,0:T(8,128)(2,1)S(1)}, bf16[256,4096]{1,0:T(8,128)(2,1)}, u32[]{:S(2)}) copy-start(bf16[256,4096]{1,0:T(8,128)(2,1)} %param.11) | copy-start | bytes 6291460
  7.2 278.7 %all-gather.6.cloned.1.call-start = ((), (), s32[]{:S(2)}) async-start(), calls=%async_computation.6 | async-start | bytes 5242880 | tf_op jit(solution)/shard_map/all_gather | solution.py:239
  7.9 277.9 %all-gather.8.cloned.1.call-start = ((), (), s32[]{:S(2)}) async-start(), calls=%async_computation.7 | async-start | bytes 5242880 | tf_op jit(solution)/shard_map/all_gather | solution.py:240
  8.7 5.7 %collective-permute-start.1 = (s32[2,256]{1,0:T(2,128)S(1)}, s32[2,256]{1,0:T(2,128)S(1)}, u32[]{:S(2)}, u32[]{:S(2)}) collective-permute-start(s32[2,256]{1,0:T(2,128)S(1)} %bitcast.67), channel_id=1, source_target_pairs={{0,4},{1,5},{2,6},{3,7},{4,0},{5,1},{6,2},{7,3},{8,12},{9,13},{10,... | collective-permute-start | bytes 6152 | tf_op jit(solution)/shard_map/ppermute | solution.py:213
  17.7 105.3 %all-to-all-start.3 = ((bf16[4,96,4096]{2,1,0:T(8,128)(2,1)}), bf16[4,96,4096]{2,1,0:T(8,128)(2,1)S(1)}, u32[]{:S(2)}, u32[]{:S(2)}) async-start(bf16[4,96,4096]{2,1,0:T(8,128)(2,1)} %bitcast.64), calls=%async_computation.3 | async-start | bytes 6291456 | tf_op jit(solution)/shard_map/all_to_all | solution.py:221
  21.8 297.1 %all-gather.10.cloned.1.call-start = ((), (), s32[]{:S(2)}) async-start(), calls=%async_computation.9 | async-start | bytes 7864320 | tf_op jit(solution)/shard_map/all_gather | solution.py:241
  26.6 92.4 %collective-permute-start = (bf16[256,4096]{0,1:T(8,128)(2,1)}, bf16[256,4096]{0,1:T(8,128)(2,1)S(1)}, u32[]{:S(2)}, u32[]{:S(2)}) collective-permute-start(bf16[256,4096]{0,1:T(8,128)(2,1)} %copy.35), channel_id=1, source_target_pairs={{0,4},{1,5},{2,6},{3,7},{4,0},{5,1},{6,2},{7,3},{8,12},{9,13},{10,... | collective-permute-start | bytes 6291464 | tf_op jit(solution)/shard_map/ppermute | solution.py:212
  119.0 1.4 copy-start.10
  123.0 72.3 %copy-start.4 = (bf16[4,96,4096]{2,1,0:T(8,128)(2,1)}, bf16[4,96,4096]{2,1,0:T(8,128)(2,1)S(1)}, u32[]{:S(2)}) copy-start(bf16[4,96,4096]{2,1,0:T(8,128)(2,1)S(1)} %all-to-all-done.3) | copy-start | bytes 9437188
  123.0 4.8 %copy-start.16 = (bf16[256,2]{0,1:T(2,128)(2,1)S(1)}, bf16[256,2]{0,1:T(2,128)(2,1)}, u32[]{:S(2)}) copy-start(bf16[256,2]{0,1:T(2,128)(2,1)} %param.16) | copy-start | bytes 3076
  123.0 72.2 %all-to-all-start.4 = ((bf16[4,96,4096]{2,1,0:T(8,128)(2,1)}), bf16[4,96,4096]{2,1,0:T(8,128)(2,1)}, u32[]{:S(2)}, u32[]{:S(2)}) async-start(bf16[4,96,4096]{2,1,0:T(8,128)(2,1)} %bitcast.63), calls=%async_computation.4 | async-start | bytes 6291456 | tf_op jit(solution)/shard_map/all_to_all | solution.py:221
  127.8 209.0 %reduce-scatter.2.cloned.1.call-start = ((), (), s32[]{:S(2)}) async-start(), calls=%async_computation.8 | async-start | bytes 7864320 | tf_op jit(solution)/shard_map/reduce_scatter | solution.py:257
  195.3 1.3 copy-start.6
  205.5 2.6 copy-start
  208.1 6.0 %copy-start.11 = (bf16[256,4096]{0,1:T(8,128)(2,1)S(1)}, bf16[256,4096]{0,1:T(8,128)(2,1)}, u32[]{:S(2)}) copy-start(bf16[256,4096]{0,1:T(8,128)(2,1)} %copy-done.10) | copy-start | bytes 6291460
  210.6 17.5 %all-to-all-start.1 = ((bf16[4,256,512]{1,2,0:T(8,128)(2,1)}), bf16[4,256,512]{1,2,0:T(8,128)(2,1)S(1)}, u32[]{:S(2)}, u32[]{:S(2)}) async-start(bf16[4,256,512]{1,2,0:T(8,128)(2,1)} %bitcast.4), calls=%async_computation.1 | async-start | bytes 2097152 | tf_op jit(solution)/shard_map/all_to_all | solution.py:227
  228.0 6.8 %copy-start.12 = (bf16[4,256,512]{1,2,0:T(8,128)(2,1)}, bf16[4,256,512]{1,2,0:T(8,128)(2,1)S(1)}, u32[]{:S(2)}) copy-start(bf16[4,256,512]{1,2,0:T(8,128)(2,1)S(1)} %all-to-all-done.1) | copy-start | bytes 3145732
  228.0 25.4 %all-to-all-start.2 = ((bf16[4,256,512]{1,2,0:T(8,128)(2,1)}), bf16[4,256,512]{1,2,0:T(8,128)(2,1)S(1)}, u32[]{:S(2)}, u32[]{:S(2)}) async-start(bf16[4,256,512]{1,2,0:T(8,128)(2,1)} %bitcast.7), calls=%async_computation.2 | async-start | bytes 2097152 | tf_op jit(solution)/shard_map/all_to_all | solution.py:227
  253.4 1.0 copy-start.13
  253.4 5.0 %copy-start.15 = (s32[16,4]{0,1:T(4,128)S(1)}, s32[16,4]{0,1:T(4,128)}, u32[]{:S(2)}) copy-start(s32[16,4]{0,1:T(4,128)} %param.14) | copy-start | bytes 772
  254.4 31.5 %all-to-all-start = ((bf16[8,256,512]{2,1,0:T(8,128)(2,1)}), bf16[8,256,512]{2,1,0:T(8,128)(2,1)S(1)}, u32[]{:S(2)}, u32[]{:S(2)}) async-start(bf16[8,256,512]{2,1,0:T(8,128)(2,1)} %bitcast.65), calls=%async_computation | async-start | bytes 4194304 | tf_op jit(solution)/shard_map/all_to_all | solution.py:234
  285.8 2.2 copy-start.1
  288.0 2.2 copy-start.2
  290.2 1.2 copy-start.3
  319.0 1.9 copy-start.5
  320.8 1.3 copy-start.7
  322.1 1.3 copy-start.8
Sparse Core Ops, SparseCore 0:
  9.6 37.1 all-gather.5
  48.3 34.4 all-gather.7
  84.4 46.3 all-gather.9
  208.2 56.3 reduce-scatter.1

commit v2 on v1

--- a/solution.py
+++ b/solution.py
@@ -6,6 +6,7 @@
 from jax.experimental import pallas as pl
 from jax.experimental.pallas import tpu as pltpu
 from jax.sharding import PartitionSpec as P
+
 
 HD = 128
 QBLK = 128
@@ -77,18 +78,19 @@
     o_ref[...] = total.astype(o_ref.dtype)
 
 
-def down_terms(weighted_t, near, far):
+def down_terms(weighted_t, near, far, part):
     ff, slots = weighted_t.shape
-    cut, width = near.shape
+    cut, width = far.shape
     tile = min(1024, width)
+    first = part * (width // tile)
     return pl.pallas_call(
         down_kernel,
         out_shape=jax.ShapeDtypeStruct((ff, width), jnp.bfloat16),
         grid=(width // tile,),
         in_specs=[
             pl.BlockSpec((ff, slots), lambda i: (0, 0)),
+            pl.BlockSpec((slots - cut, tile), lambda i: (0, i + first)),
             pl.BlockSpec((cut, tile), lambda i: (0, i)),
-            pl.BlockSpec((slots - cut, tile), lambda i: (0, i)),
         ],
         out_specs=pl.BlockSpec((ff, tile), lambda i: (0, i)),
         compiler_params=pltpu.CompilerParams(vmem_limit_bytes=40 * 2**20),
@@ -101,7 +103,7 @@
 
 
 def slot_kernel(
-    half_ref, near_ref, far_ref, w_ref, gate_ref, up_ref, sw_ref, gg_ref, ug_ref, cg_ref, acc
+    half_ref, near_ref, far_a_ref, far_b_ref, w_ref, gate_ref, up_ref, sw_ref, gg_ref, ug_ref, cg_ref, acc
 ):
     step = pl.program_id(0)
     cut = near_ref.shape[0]
@@ -112,7 +114,8 @@
 
     w = w_ref[...]
     acc[:cut, :] += lax.dot_general(near_ref[...], w, DOT_NT, preferred_element_type=jnp.float32)
-    acc[cut:, :] += lax.dot_general(far_ref[...], w, DOT_NT, preferred_element_type=jnp.float32)
+    far = jnp.where(step < pl.num_programs(0) // 2, far_a_ref[...], far_b_ref[...])
+    acc[cut:, :] += lax.dot_general(far, w, DOT_NT, preferred_element_type=jnp.float32)
 
     @pl.when(step == pl.num_programs(0) - 1)
     def _():
@@ -132,10 +135,11 @@
             ug_ref[rows, :] = (hidden_grad * silu).astype(jnp.bfloat16)
 
 
-def slot_grads(my_half, near, far, weights, gate, up, slot_weight):
+def slot_grads(my_half, near, far_a, far_b, weights, gate, up, slot_weight):
     cut, width = near.shape
     slots, ff = gate.shape
-    tile = min(512, width)
+    tile = min(512, width // 2)
+    per_part = width // 2 // tile
 
     def full(shape):
         return pl.BlockSpec(shape, lambda i, *_: (0, 0), pipeline_mode=pl.Buffered(1))
@@ -152,7 +156,8 @@
             grid=(width // tile,),
             in_specs=[
                 pl.BlockSpec((cut, tile), lambda i, *_: (0, i)),
-                pl.BlockSpec((slots - cut, tile), lambda i, *_: (0, i)),
+                pl.BlockSpec((slots - cut, tile), lambda i, *_: (0, jnp.minimum(i, per_part - 1))),
+                pl.BlockSpec((slots - cut, tile), lambda i, *_: (0, jnp.maximum(i - per_part, 0))),
                 pl.BlockSpec((ff, tile), lambda i, *_: (0, i)),
                 full((slots, ff)),
                 full((slots, ff)),
@@ -171,7 +176,7 @@
             bytes_accessed=2 * (4 * ff * slots + slots * width + ff * width),
             transcendentals=slots * ff,
         ),
-    )(my_half, near, far, weights, gate, up, slot_weight)
+    )(my_half, near, far_a, far_b, weights, gate, up, slot_weight)
 
 
 def before_count(hits):
@@ -199,7 +204,7 @@
     me = lax.axis_index("expert")
     my_half = me // half
     tokens, width = out_grad.shape
-    slots, ff = gate_pre.shape[1:]
+    slots, _ = gate_pre.shape[1:]
     capacity = slots // experts
     head_cols = width // experts
     groups = [list(range(half)), list(range(half, experts))]
@@ -209,32 +214,52 @@
     packed = jnp.concatenate([routes_t.astype(jnp.float32), combine.T.astype(jnp.float32)], axis=0)
     topk = routes_t.shape[0]
 
-    far_grad = lax.ppermute(out_grad, "expert", partner)
-    far_routes = lax.ppermute(routes_t, "expert", partner)
     packed_all = lax.all_gather(packed, "expert", axis=0, tiled=False)
 
+    def after(value, earlier):
+        return lax.optimization_barrier((value, earlier))[0]
+
+    def swap(rows, groups_used):
+        return lax.all_to_all(
+            rows, "expert", split_axis=0, concat_axis=0, axis_index_groups=groups_used, tiled=True
+        )
+
+    part_cols = width // 2
+    far_a = lax.ppermute(after(out_grad[:, :part_cols], packed_all), "expert", partner)
+    far_b = lax.ppermute(after(out_grad[:, part_cols:], far_a), "expert", partner)
+    other = lax.rem(me + half, experts)
+    far_routes = lax.dynamic_index_in_dim(packed_all, other, 0, keepdims=False)[:topk]
     here = my_half * half + jnp.arange(half, dtype=jnp.int32)
 
-    def exchange(rows, rows_routes):
-        placing = placing_of(rows_routes, here, capacity)
+    def pick(placing, rows):
         picked = jnp.dot(placing, rows, preferred_element_type=jnp.float32).astype(jnp.bfloat16)
-        slot_rows = lax.all_to_all(
-            picked.reshape(half, capacity, width), "expert", split_axis=0, concat_axis=0,
-            axis_index_groups=groups, tiled=True,
-        ).reshape(half * capacity, width)
-        columns = lax.dynamic_slice_in_dim(rows, my_half * half * head_cols, half * head_cols, 1)
-        columns = columns.reshape(tokens, half, head_cols).transpose(1, 0, 2)
-        columns = lax.all_to_all(
-            columns, "expert", split_axis=0, concat_axis=0, axis_index_groups=groups, tiled=True
-        ).reshape(half * tokens, head_cols)
-        return slot_rows, columns
-
-    near_rows, near_cols = exchange(out_grad, routes_t)
-    far_rows, far_cols = exchange(far_grad, far_routes)
-    head_queries = lax.all_to_all(
-        queries.reshape(tokens, experts, head_cols).transpose(1, 0, 2),
-        "expert", split_axis=0, concat_axis=0, tiled=True,
-    ).reshape(experts * tokens, head_cols)
+        return picked.reshape(half, capacity, rows.shape[1])
+
+    def columns_of(rows):
+        return jnp.stack([rows[:, r * head_cols : (r + 1) * head_cols] for r in range(half)])
+
+    near_placing = placing_of(routes_t, here, capacity)
+    far_placing = placing_of(far_routes, here.astype(jnp.float32), capacity)
+    upper = my_half == 1
+    near_own = columns_of(jnp.where(upper, out_grad[:, part_cols:], out_grad[:, :part_cols]))
+    far_own = columns_of(jnp.where(upper, far_b, far_a))
+
+    near_slots = pick(near_placing, out_grad)
+    near_rows = swap(near_slots, groups)
+    near_cols = swap(after(near_own, near_rows), groups)
+    slots_a = after(pick(far_placing, far_a), near_cols)
+    rows_a = swap(slots_a, groups)
+    rows_b = swap(after(pick(far_placing, far_b), rows_a), groups)
+    far_cols = swap(after(far_own, rows_b), groups)
+    by_head = jnp.stack(
+        [queries[:, r * head_cols : (r + 1) * head_cols] for r in range(experts)]
+    )
+    head_queries = swap(after(by_head, far_cols), None).reshape(experts * tokens, head_cols)
+    near_rows = near_rows.reshape(half * capacity, width)
+    rows_a = rows_a.reshape(half * capacity, part_cols)
+    rows_b = rows_b.reshape(half * capacity, part_cols)
+    near_cols = near_cols.reshape(half * tokens, head_cols)
+    far_cols = far_cols.reshape(half * tokens, head_cols)
 
     keys = lax.all_gather(mem_keys, "mem", axis=0, tiled=True)
     values = lax.all_gather(mem_values, "mem", axis=0, tiled=True)
@@ -254,13 +279,17 @@
     swapped = jnp.roll(weighted, half * capacity, axis=0)
     weighted_t = jnp.where(my_half == 0, weighted, swapped).T
 
-    w_down_grad = lax.psum_scatter(
-        down_terms(weighted_t, near_rows, far_rows), "mem", scatter_dimension=0, tiled=True
-    )[None]
+    down = [
+        lax.psum_scatter(
+            down_terms(weighted_t, near_rows, far, part), "mem", scatter_dimension=0, tiled=True
+        )
+        for part, far in enumerate((rows_a, rows_b))
+    ]
+    w_down_grad = jnp.concatenate(down, axis=1)[None]
     side = my_half.astype(jnp.int32).reshape(1)
     query_grad = attend(block_index, side, head_queries, near_cols, far_cols, keys, values)
     gate_grad, up_grad, combine_grad = slot_grads(
-        side, near_rows, far_rows, weights, gate_pre[0], up_pre[0], slot_weight
+        side, near_rows, rows_a, rows_b, weights, gate_pre[0], up_pre[0], slot_weight
     )
     return (
         query_grad, w_down_grad, gate_grad[None], up_grad[None], combine_grad.reshape(1, slots)
@@ -287,6 +316,7 @@
         P("expert", "mem", None),
         P("expert", "mem"),
     )
+
     return jax.shard_map(
         per_device, mesh=mesh, in_specs=in_specs, out_specs=out_specs, check_vma=False
     )

time: 345 us -> 364 us (1.055)
  waiting for transfers between devices: 148 us -> 178 us
  blocking collectives: 60.6 us -> 32.4 us
  other arithmetic: 4.52 us -> 14.9 us
  starting transfers between devices: 26.7 us -> 31 us
    all_to_all x5 -> x6, waiting for transfers between devices: 55 us -> 85 us  [swap(): lax.all_to_all(rows, 'expert', split_axis=0, concat_axis=0, axis_index_gr...]
    all_gather x1, blocking collectives: 60.6 us -> 32.4 us  [per_device(): packed_all = lax.all_gather(packed, 'expert', axis=0, tiled=False)]
    unnamed x36 -> x38, local copies, waits for them, and re-layouts: 20.4 us -> 27.3 us
    all_to_all x5 -> x6, starting transfers between devices: 19.8 us -> 26.2 us  [swap(): lax.all_to_all(rows, 'expert', split_axis=0, concat_axis=0, axis_index_gr...]
    select_n x0 -> x2, other arithmetic: none -> 4.48 us  [the longest x1 3.13 us: per_device(): jnp.where(upper, out_grad[:, part_cols:], out_grad[:, :part_cols])]
    all_to_all x2 -> x0, local copies, waits for them, and re-layouts: 3.77 us -> none  [exchange(): lax.all_to_all(columns, 'expert', split_axis=0, concat_axis=0, axis_index...]
    pallas_call x1 -> x2, Pallas kernels: 8.92 us -> 10 us  [down_terms(): pl.pallas_call(down_kernel, out_shape=jax.ShapeDtypeStruct((ff, width), j...]
  transfers between devices with their start and end apart: 11 -> 13, of which waited for: 5 -> 7; matrix products, arithmetic and copies ran while one was open for 8% -> 10% of each run, Pallas kernels for 14% -> 14%
where the time goes in v2:
time: 364 us; the launch traced here: 362 us
  waiting for transfers between devices  178 us (49%)
  Pallas kernels  52.2 us (14%)
  local copies, waits for them, and re-layouts  32.6 us (9%)
  blocking collectives  32.4 us (9%)
  starting transfers between devices  31 us (9%)
  other arithmetic  14.9 us (4%)
  between operations  14 us (4%)
  matrix products  6.53 us (2%)
    all_to_all x6, waiting for transfers between devices, swap(): lax.all_to_all(rows, 'expert', split_axis=0, concat_axis=0, axis_index_gr...  85 us
    ppermute x1, waiting for transfers between devices, per_device(): lax.ppermute(after(out_grad[:, :part_cols], packed_all), 'expert', partner)  46.1 us
    ppermute x1, waiting for transfers between devices, per_device(): lax.ppermute(after(out_grad[:, part_cols:], far_a), 'expert', partner)  45.2 us
    all_gather x1, blocking collectives, per_device(): packed_all = lax.all_gather(packed, 'expert', axis=0, tiled=False)  32.4 us
    pallas_call x1, Pallas kernels, attend(): pl.pallas_call(attend_kernel, out_shape=jax.ShapeDtypeStruct((rows, width...  29.3 us
    unnamed x38, local copies, waits for them, and re-layouts  27.3 us
    all_to_all x6, starting transfers between devices, swap(): lax.all_to_all(rows, 'expert', split_axis=0, concat_axis=0, axis_index_gr...  26.2 us
    pallas_call x1, Pallas kernels, slot_grads(): pl.pallas_call(slot_kernel, out_shape=(jax.ShapeDtypeStruct((slots, ff),...  12.9 us
  transfers between devices with their start and end apart: 13, of which 7 were waited for; matrix products, arithmetic and copies ran while one was open for 10% of the time, Pallas kernels for 14%

profile of v2, /device:TPU:0, one launch (start us, length us, event | category | flops | bytes accessed | tf_op | source)
XLA Modules:
  0.0 362.2 jit_solution(6489283377206761177)
XLA Ops:
  8.8 32.4 %all-gather.1 = f32[8,4,256]{2,1,0:T(4,128)S(1)} all-gather(f32[1,4,256]{2,1,0:T(4,128)S(1)} %maximum_bitcast_fusion.1), channel_id=2, replica_groups=mesh['mem'=4,'expert'=8] {'expert'}, dimensions={0}, use_global_device_ids=true | all-gather | bytes 36864 | tf_op jit(solution)/shard_map/all_gather | solution.py:217
  42.0 2.6 convolution_convert_fusion
  44.6 3.7 %all-to-all-start = ((bf16[4,96,4096]{2,1,0:T(8,128)(2,1)}), bf16[4,96,4096]{2,1,0:T(8,128)(2,1)S(1)}, u32[]{:S(2)}, u32[]{:S(2)}) async-start(bf16[4,96,4096]{2,1,0:T(8,128)(2,1)} %bitcast.87), calls=%async_computation | async-start | bytes 6291456 | tf_op jit(solution)/shard_map/all_to_all | solution.py:223
  49.0 3.1 broadcast_select_fusion
  52.3 1.1 pad_maximum_fusion.1
  53.4 25.1 %all-to-all-done = bf16[4,96,4096]{2,1,0:T(8,128)(2,1)S(1)} async-done(((bf16[4,96,4096]{2,1,0:T(8,128)(2,1)}), bf16[4,96,4096]{2,1,0:T(8,128)(2,1)S(1)}, u32[]{:S(2)}, u32[]{:S(2)}) %all-to-all-start) | async-done | bytes 3145760 | tf_op jit(solution)/shard_map/all_to_all | solution.py:223
  78.4 4.2 %all-to-all-start.1 = ((bf16[4,256,512]{2,1,0:T(8,128)(2,1)}), bf16[4,256,512]{2,1,0:T(8,128)(2,1)}, u32[]{:S(2)}, u32[]{:S(2)}) async-start(bf16[4,256,512]{2,1,0:T(8,128)(2,1)} %pad_maximum_fusion.1), calls=%async_computation.1 | async-start | bytes 2097152 | tf_op jit(solution)/shard_map/all_to_all | solution.py:223
  82.7 2.0 collective-permute-start
  84.7 46.1 %collective-permute-done = bf16[256,2048]{1,0:T(8,128)(2,1)S(1)} collective-permute-done((bf16[256,2048]{1,0:T(8,128)(2,1)}, bf16[256,2048]{1,0:T(8,128)(2,1)S(1)}, u32[]{:S(2)}, u32[]{:S(2)}) %collective-permute-start) | collective-permute-done | bytes 1048608 | tf_op jit(solution)/shard_map/ppermute | solution.py:228
  131.9 1.7 convolution_convert_fusion.1
  133.6 4.3 %all-to-all-start.2 = ((bf16[4,96,2048]{2,1,0:T(8,128)(2,1)}), bf16[4,96,2048]{2,1,0:T(8,128)(2,1)}, u32[]{:S(2)}, u32[]{:S(2)}) async-start(bf16[4,96,2048]{2,1,0:T(8,128)(2,1)} %bitcast.88), calls=%async_computation.2 | async-start | bytes 3145728 | tf_op jit(solution)/shard_map/all_to_all | solution.py:223
  138.6 2.4 fusion.5
  141.0 1.3 fusion.6
  142.4 2.4 copy.27.wt_ref
  144.7 11.6 %all-to-all-done.2 = bf16[4,96,2048]{2,1,0:T(8,128)(2,1)} async-done(((bf16[4,96,2048]{2,1,0:T(8,128)(2,1)}), bf16[4,96,2048]{2,1,0:T(8,128)(2,1)}, u32[]{:S(2)}, u32[]{:S(2)}) %all-to-all-start.2) | async-done | bytes 1572896 | tf_op jit(solution)/shard_map/all_to_all | solution.py:223
  156.3 1.3 copy-done.2
  157.6 5.0 %shard_map.138 = bf16[768,2048]{1,0:T(8,128)(2,1)S(1)} custom-call(bf16[768,768]{1,0:T(8,128)(2,1)S(1)} %copy-done.2, bf16[384,4096]{1,0:T(8,128)(2,1)S(1)} %bitcast.82, bf16[384,2048]{1,0:T(8,128)(2,1)} %bitcast.35.far_ref.far_a_ref), custom_call_target="tpu_custom_call" | custom-call | flops 2415919104 | bytes 7471104 | tf_op jit(solution)/shard_map/pallas_call | solution.py:86
  162.6 1.6 copy-done
  164.3 2.6 collective-permute-start.1
  166.8 45.2 %collective-permute-done.1 = bf16[256,2048]{1,0:T(8,128)(2,1)S(1)} collective-permute-done((bf16[256,2048]{1,0:T(8,128)(2,1)}, bf16[256,2048]{1,0:T(8,128)(2,1)S(1)}, u32[]{:S(2)}, u32[]{:S(2)}) %collective-permute-start.1) | collective-permute-done | bytes 1048608 | tf_op jit(solution)/shard_map/ppermute | solution.py:229
  213.0 1.7 convolution_convert_fusion.2
  214.7 4.4 %all-to-all-start.3 = ((bf16[4,96,2048]{2,1,0:T(8,128)(2,1)}), bf16[4,96,2048]{2,1,0:T(8,128)(2,1)}, u32[]{:S(2)}, u32[]{:S(2)}) async-start(bf16[4,96,2048]{2,1,0:T(8,128)(2,1)} %bitcast.89), calls=%async_computation.3 | async-start | bytes 3145728 | tf_op jit(solution)/shard_map/all_to_all | solution.py:223
  219.2 1.7 bitcast_dynamic-update-slice_fusion.7
  220.8 16.3 %all-to-all-done.3 = bf16[4,96,2048]{2,1,0:T(8,128)(2,1)} async-done(((bf16[4,96,2048]{2,1,0:T(8,128)(2,1)}), bf16[4,96,2048]{2,1,0:T(8,128)(2,1)}, u32[]{:S(2)}, u32[]{:S(2)}) %all-to-all-start.3) | async-done | bytes 1572896 | tf_op jit(solution)/shard_map/all_to_all | solution.py:223
  237.1 1.3 copy-done.3
  238.4 5.0 %shard_map.139 = bf16[768,2048]{1,0:T(8,128)(2,1)S(1)} custom-call(bf16[768,768]{1,0:T(8,128)(2,1)S(1)} %copy-done.3, bf16[384,4096]{1,0:T(8,128)(2,1)S(1)} %bitcast.83, bf16[384,2048]{1,0:T(8,128)(2,1)} %bitcast.36.far_ref.far_b_ref), custom_call_target="tpu_custom_call" | custom-call | flops 2415919104 | bytes 7471104 | tf_op jit(solution)/shard_map/pallas_call | solution.py:86
  243.4 1.6 copy-done.1
  245.0 1.4 broadcast_select_fusion.1
  246.5 1.1 pad_maximum_fusion
  247.6 4.3 %all-to-all-start.4 = ((bf16[4,256,512]{2,1,0:T(8,128)(2,1)}), bf16[4,256,512]{2,1,0:T(8,128)(2,1)}, u32[]{:S(2)}, u32[]{:S(2)}) async-start(bf16[4,256,512]{2,1,0:T(8,128)(2,1)} %pad_maximum_fusion), calls=%async_computation.4 | async-start | bytes 2097152 | tf_op jit(solution)/shard_map/all_to_all | solution.py:223
  251.8 1.7 bitcast_dynamic-update-slice_fusion.6
  253.6 1.7 bitcast_dynamic-update-slice_fusion.5
  255.3 1.7 bitcast_dynamic-update-slice_fusion.4
  256.9 1.7 bitcast_dynamic-update-slice_fusion.3
  258.6 1.7 bitcast_dynamic-update-slice_fusion.2
  260.3 1.7 bitcast_dynamic-update-slice_fusion.1
  262.0 1.7 bitcast_dynamic-update-slice_fusion
  263.7 2.0 all-to-all-done.4
  265.6 5.2 %all-to-all-start.5 = ((bf16[8,256,512]{2,1,0:T(8,128)(2,1)}), bf16[8,256,512]{2,1,0:T(8,128)(2,1)}, u32[]{:S(2)}, u32[]{:S(2)}) async-start(bf16[8,256,512]{2,1,0:T(8,128)(2,1)} %bitcast_dynamic-update-slice_fusion), calls=%async_computation.5 | async-start | bytes 4194304 | tf_op jit(solution)/shard_map/all_to_all | solution.py:223
  271.2 1.3 copy-done.6
  272.5 1.3 copy-done.7
  273.8 12.9 %shard_map.140 = (bf16[768,768]{1,0:T(8,128)(2,1)}, bf16[768,768]{1,0:T(8,128)(2,1)}, f32[768,1]{1,0:T(8,128)S(1)}) custom-call(s32[1]{0:T(128)} %bitcast.half_ref, bf16[384,4096]{1,0:T(8,128)(2,1)S(1)} %bitcast.84, bf16[384,2048]{1,0:T(8,128)(2,1)} %bitcast.35.far_ref.far_a_ref, bf16[384,2048]{1,0:T(8,128)(2,1)} %bitcast.36.far_ref.far_b_ref, ...), custom_call_target="tpu_custom_call" | custom-call | flops 4831838208 | bytes 17301504 | tf_op jit(solution)/shard_map/pallas_call | solution.py:147
  287.4 1.2 reduce
  289.2 30.2 %all-to-all-done.5 = bf16[8,256,512]{2,1,0:T(8,128)(2,1)} async-done(((bf16[8,256,512]{2,1,0:T(8,128)(2,1)}), bf16[8,256,512]{2,1,0:T(8,128)(2,1)}, u32[]{:S(2)}, u32[]{:S(2)}) %all-to-all-start.5) | async-done | bytes 2097184 | tf_op jit(solution)/shard_map/all_to_all | solution.py:223
  319.3 2.2 copy-done.4
  321.5 2.2 copy-done.5
  323.7 29.3 %shard_map.137 = bf16[2048,512]{1,0:T(8,128)(2,1)} custom-call(s32[16,4]{1,0:T(8,128)S(1)} %copy.26.idx_ref, s32[1]{0:T(128)} %bitcast.half_ref, bf16[2048,512]{1,0:T(8,128)(2,1)} %bitcast.28.q_ref, bf16[1024,512]{1,0:T(8,128)(2,1)} %bitcast.29.near_ref, bf16[1024,512]{1,0:T(8,128)(2,1)} %bitcast.30.far_ref, bf16[4096,512]{1,0:T(8,128)(2,1)S(1)} %copy-done.4, ...), custom_call_target="tpu_custom_call" | custom-call | flops 3221225472 | bytes 14680064 | tf_op jit(solution)/shard_map/pallas_call | solution.py:50
  353.0 2.7 maximum_bitcast_fusion
  (61 shorter events, 7.5 us)
Async XLA Ops:
  7.2 1.6 copy-start.14
  7.2 1.6 copy-start.12
  7.2 34.8 %copy-start.9 = (bf16[256,4096]{1,0:T(8,128)(2,1)S(1)}, bf16[256,4096]{1,0:T(8,128)(2,1)}, u32[]{:S(2)}) copy-start(bf16[256,4096]{1,0:T(8,128)(2,1)} %param.11) | copy-start | bytes 6291460
  7.2 264.0 %all-gather.10.cloned.1.call-start = ((), (), s32[]{:S(2)}) async-start(), calls=%async_computation.12 | async-start | bytes 7864320 | tf_op jit(solution)/shard_map/all_gather | solution.py:266
  7.9 281.2 %all-gather.6.cloned.1.call-start = ((), (), s32[]{:S(2)}) async-start(), calls=%async_computation.8 | async-start | bytes 5242880 | tf_op jit(solution)/shard_map/all_gather | solution.py:264
  44.6 33.8 %all-to-all-start = ((bf16[4,96,4096]{2,1,0:T(8,128)(2,1)}), bf16[4,96,4096]{2,1,0:T(8,128)(2,1)S(1)}, u32[]{:S(2)}, u32[]{:S(2)}) async-start(bf16[4,96,4096]{2,1,0:T(8,128)(2,1)} %bitcast.87), calls=%async_computation | async-start | bytes 6291456 | tf_op jit(solution)/shard_map/all_to_all | solution.py:223
  48.3 240.9 %all-gather.8.cloned.1.call-start = ((), (), s32[]{:S(2)}) async-start(), calls=%async_computation.9 | async-start | bytes 5242880 | tf_op jit(solution)/shard_map/all_gather | solution.py:265
  78.4 55.2 %all-to-all-start.1 = ((bf16[4,256,512]{2,1,0:T(8,128)(2,1)}), bf16[4,256,512]{2,1,0:T(8,128)(2,1)}, u32[]{:S(2)}, u32[]{:S(2)}) async-start(bf16[4,256,512]{2,1,0:T(8,128)(2,1)} %pad_maximum_fusion.1), calls=%async_computation.1 | async-start | bytes 2097152 | tf_op jit(solution)/shard_map/all_to_all | solution.py:223
  82.7 48.2 %collective-permute-start = (bf16[256,2048]{1,0:T(8,128)(2,1)}, bf16[256,2048]{1,0:T(8,128)(2,1)S(1)}, u32[]{:S(2)}, u32[]{:S(2)}) collective-permute-start(bf16[256,2048]{1,0:T(8,128)(2,1)} %get-tuple-element.15), channel_id=1, source_target_pairs={{0,4},{1,5},{2,6},{3,7},{4,0},{5,1},{6,2},{7,3},{8,12},{9,13},{10,... | collective-permute-start | bytes 3145736 | tf_op jit(solution)/shard_map/ppermute | solution.py:228
  130.9 1.0 copy-start.10
  133.6 22.7 %all-to-all-start.2 = ((bf16[4,96,2048]{2,1,0:T(8,128)(2,1)}), bf16[4,96,2048]{2,1,0:T(8,128)(2,1)}, u32[]{:S(2)}, u32[]{:S(2)}) async-start(bf16[4,96,2048]{2,1,0:T(8,128)(2,1)} %bitcast.88), calls=%async_computation.2 | async-start | bytes 3145728 | tf_op jit(solution)/shard_map/all_to_all | solution.py:223
  138.0 215.0 %reduce-scatter.3.cloned.1.call-start = ((), (), s32[]{:S(2)}) async-start(), calls=%async_computation.10 | async-start | bytes 3932160 | tf_op jit(solution)/shard_map/reduce_scatter | solution.py:283
  156.3 1.3 copy-start.2
  162.6 1.6 copy-start
  164.3 47.8 %collective-permute-start.1 = (bf16[256,2048]{1,0:T(8,128)(2,1)}, bf16[256,2048]{1,0:T(8,128)(2,1)S(1)}, u32[]{:S(2)}, u32[]{:S(2)}) collective-permute-start(bf16[256,2048]{1,0:T(8,128)(2,1)} %get-tuple-element.16), channel_id=1, source_target_pairs={{0,4},{1,5},{2,6},{3,7},{4,0},{5,1},{6,2},{7,3},{8,12},{9,13},{10,... | collective-permute-start | bytes 3145736 | tf_op jit(solution)/shard_map/ppermute | solution.py:229
  212.0 1.0 copy-start.11
  214.7 22.4 %all-to-all-start.3 = ((bf16[4,96,2048]{2,1,0:T(8,128)(2,1)}), bf16[4,96,2048]{2,1,0:T(8,128)(2,1)}, u32[]{:S(2)}, u32[]{:S(2)}) async-start(bf16[4,96,2048]{2,1,0:T(8,128)(2,1)} %bitcast.89), calls=%async_computation.3 | async-start | bytes 3145728 | tf_op jit(solution)/shard_map/all_to_all | solution.py:223
  219.1 133.9 %reduce-scatter.5.cloned.1.call-start = ((), (), s32[]{:S(2)}) async-start(), calls=%async_computation.11 | async-start | bytes 3932160 | tf_op jit(solution)/shard_map/reduce_scatter | solution.py:283
  237.1 1.3 copy-start.3
  243.4 1.6 copy-start.1
  247.6 18.1 %all-to-all-start.4 = ((bf16[4,256,512]{2,1,0:T(8,128)(2,1)}), bf16[4,256,512]{2,1,0:T(8,128)(2,1)}, u32[]{:S(2)}, u32[]{:S(2)}) async-start(bf16[4,256,512]{2,1,0:T(8,128)(2,1)} %pad_maximum_fusion), calls=%async_computation.4 | async-start | bytes 2097152 | tf_op jit(solution)/shard_map/all_to_all | solution.py:223
  263.7 7.5 %copy-start.13 = (s32[16,4]{0,1:T(4,128)S(1)}, s32[16,4]{0,1:T(4,128)}, u32[]{:S(2)}) copy-start(s32[16,4]{0,1:T(4,128)} %param.14) | copy-start | bytes 772
  265.6 53.7 %all-to-all-start.5 = ((bf16[8,256,512]{2,1,0:T(8,128)(2,1)}), bf16[8,256,512]{2,1,0:T(8,128)(2,1)}, u32[]{:S(2)}, u32[]{:S(2)}) async-start(bf16[8,256,512]{2,1,0:T(8,128)(2,1)} %bitcast_dynamic-update-slice_fusion), calls=%async_computation.5 | async-start | bytes 4194304 | tf_op jit(solution)/shard_map/all_to_all | solution.py:223
  271.2 1.3 copy-start.6
  272.5 1.3 copy-start.7
  286.6 0.7 copy-start.8
  319.3 2.2 copy-start.4
  321.5 2.2 copy-start.5
Sparse Core Ops, SparseCore 0:
  9.6 49.0 all-gather.9
  60.2 34.4 all-gather.5
  96.3 34.4 all-gather.7
  164.4 37.1 reduce-scatter.2
  245.1 37.8 reduce-scatter.4

commit v3 on v2

--- a/solution.py
+++ b/solution.py
@@ -13,16 +13,16 @@
 DOT_NT = (((1,), (1,)), ((), ()))
 
 
-def attend_kernel(idx_ref, half_ref, q_ref, near_ref, far_ref, k_ref, v_ref, o_ref):
+def attend_kernel(idx_ref, half_ref, nq_ref, fq_ref, near_ref, far_ref, k_ref, v_ref, o_ref):
     b = pl.program_id(0)
     side = b // (pl.num_programs(0) // 2)
     is_near = side == half_ref[0]
     ksel = idx_ref.shape[1]
     scale = 1.0 / HD**0.5
     starts = [pl.multiple_of(idx_ref[b, j] * QBLK, QBLK) for j in range(ksel)]
-    for head in range(q_ref.shape[1] // HD):
+    for head in range(nq_ref.shape[1] // HD):
         cols = slice(head * HD, (head + 1) * HD)
-        q = q_ref[:, cols]
+        q = jnp.where(is_near, nq_ref[:, cols], fq_ref[:, cols])
         g = jnp.where(is_near, near_ref[:, cols], far_ref[:, cols])
         k = jnp.concatenate([k_ref[pl.ds(s, QBLK), cols] for s in starts], axis=0)
         v = jnp.concatenate([v_ref[pl.ds(s, QBLK), cols] for s in starts], axis=0)
@@ -36,15 +36,17 @@
         o_ref[:, cols] = out.astype(o_ref.dtype)
 
 
-def attend(block_index, my_half, queries, near, far, keys, values):
-    rows, width = queries.shape
+def attend(block_index, my_half, near, far, tokens, keys, values):
+    rows, width = near.shape
+    per_source = tokens // QBLK
     blocks = rows // QBLK
     per_side = blocks // 2
 
-    def side_map(b, idx, half, want_near):
+    def side_map(b, idx, half, want_near, offset):
         mine = (b // per_side) == half[0]
         use = mine if want_near else jnp.logical_not(mine)
-        return (jnp.where(use, b % per_side, 0), 0)
+        at = jnp.where(use, b % per_side, 0)
+        return (at // per_source * (2 * per_source) + at % per_source + offset, 0)
 
     whole = pl.BlockSpec(keys.shape, lambda b, *_: (0, 0), pipeline_mode=pl.Buffered(1))
     return pl.pallas_call(
@@ -54,21 +56,26 @@
             num_scalar_prefetch=2,
             grid=(blocks,),
             in_specs=[
-                pl.BlockSpec((QBLK, width), lambda b, *_: (b, 0)),
-                pl.BlockSpec((QBLK, width), functools.partial(side_map, want_near=True)),
-                pl.BlockSpec((QBLK, width), functools.partial(side_map, want_near=False)),
+                *[
+                    pl.BlockSpec(
+                        (QBLK, width),
+                        functools.partial(side_map, want_near=want_near, offset=offset),
+                    )
+                    for offset in (0, per_source)
+                    for want_near in (True, False)
+                ],
                 whole,
                 whole,
             ],
             out_specs=pl.BlockSpec((QBLK, width), lambda b, *_: (b, 0)),
         ),
-        compiler_params=pltpu.CompilerParams(vmem_limit_bytes=40 * 2**20),
+        compiler_params=pltpu.CompilerParams(vmem_limit_bytes=60 * 2**20),
         cost_estimate=pl.CostEstimate(
             flops=6 * rows * width * block_index.shape[1] * QBLK,
-            bytes_accessed=2 * (2 * keys.size + 3 * queries.size),
+            bytes_accessed=2 * (2 * keys.size + 3 * near.size),
             transcendentals=rows * width // HD * block_index.shape[1] * QBLK,
         ),
-    )(block_index, my_half, queries, near, far, keys, values)
+    )(block_index, my_half, near, far, near, far, keys, values)
 
 
 def down_kernel(wt_ref, near_ref, far_ref, o_ref):
@@ -93,7 +100,7 @@
             pl.BlockSpec((cut, tile), lambda i: (0, i)),
         ],
         out_specs=pl.BlockSpec((ff, tile), lambda i: (0, i)),
-        compiler_params=pltpu.CompilerParams(vmem_limit_bytes=40 * 2**20),
+        compiler_params=pltpu.CompilerParams(vmem_limit_bytes=60 * 2**20),
         cost_estimate=pl.CostEstimate(
             flops=2 * ff * slots * width,
             bytes_accessed=2 * (ff * slots + slots * width + ff * width),
@@ -170,7 +177,7 @@
             ),
             scratch_shapes=[pltpu.VMEM((slots, ff), jnp.float32)],
         ),
-        compiler_params=pltpu.CompilerParams(vmem_limit_bytes=40 * 2**20),
+        compiler_params=pltpu.CompilerParams(vmem_limit_bytes=60 * 2**20),
         cost_estimate=pl.CostEstimate(
             flops=2 * ff * slots * width,
             bytes_accessed=2 * (4 * ff * slots + slots * width + ff * width),
@@ -214,7 +221,7 @@
     packed = jnp.concatenate([routes_t.astype(jnp.float32), combine.T.astype(jnp.float32)], axis=0)
     topk = routes_t.shape[0]
 
-    packed_all = lax.all_gather(packed, "expert", axis=0, tiled=False)
+    far_routes = lax.ppermute(routes_t, "expert", partner)
 
     def after(value, earlier):
         return lax.optimization_barrier((value, earlier))[0]
@@ -225,10 +232,8 @@
         )
 
     part_cols = width // 2
-    far_a = lax.ppermute(after(out_grad[:, :part_cols], packed_all), "expert", partner)
+    far_a = lax.ppermute(after(out_grad[:, :part_cols], far_routes), "expert", partner)
     far_b = lax.ppermute(after(out_grad[:, part_cols:], far_a), "expert", partner)
-    other = lax.rem(me + half, experts)
-    far_routes = lax.dynamic_index_in_dim(packed_all, other, 0, keepdims=False)[:topk]
     here = my_half * half + jnp.arange(half, dtype=jnp.int32)
 
     def pick(placing, rows):
@@ -239,27 +244,35 @@
         return jnp.stack([rows[:, r * head_cols : (r + 1) * head_cols] for r in range(half)])
 
     near_placing = placing_of(routes_t, here, capacity)
-    far_placing = placing_of(far_routes, here.astype(jnp.float32), capacity)
+    far_placing = placing_of(far_routes, here, capacity)
     upper = my_half == 1
-    near_own = columns_of(jnp.where(upper, out_grad[:, part_cols:], out_grad[:, :part_cols]))
-    far_own = columns_of(jnp.where(upper, far_b, far_a))
+    low_q, high_q = queries[:, :part_cols], queries[:, part_cols:]
+    far_q = lax.ppermute(
+        after(jnp.where(upper, low_q, high_q), far_b), "expert", partner
+    )
+    own_grad = jnp.where(upper, out_grad[:, part_cols:], out_grad[:, :part_cols])
+    near_own = jnp.concatenate(
+        [columns_of(jnp.where(upper, high_q, low_q)), columns_of(own_grad)], axis=1
+    )
+    far_own = jnp.concatenate(
+        [columns_of(far_q), columns_of(jnp.where(upper, far_b, far_a))], axis=1
+    )
 
     near_slots = pick(near_placing, out_grad)
     near_rows = swap(near_slots, groups)
-    near_cols = swap(after(near_own, near_rows), groups)
+    packed_all = lax.all_gather(after(packed, near_slots), "expert", axis=0, tiled=False)
+    near_own = after(near_own, near_rows)
+    near_cols = swap(near_own, groups)
     slots_a = after(pick(far_placing, far_a), near_cols)
     rows_a = swap(slots_a, groups)
-    rows_b = swap(after(pick(far_placing, far_b), rows_a), groups)
+    slots_b = after(pick(far_placing, far_b), rows_a)
+    rows_b = swap(slots_b, groups)
     far_cols = swap(after(far_own, rows_b), groups)
-    by_head = jnp.stack(
-        [queries[:, r * head_cols : (r + 1) * head_cols] for r in range(experts)]
-    )
-    head_queries = swap(after(by_head, far_cols), None).reshape(experts * tokens, head_cols)
     near_rows = near_rows.reshape(half * capacity, width)
     rows_a = rows_a.reshape(half * capacity, part_cols)
     rows_b = rows_b.reshape(half * capacity, part_cols)
-    near_cols = near_cols.reshape(half * tokens, head_cols)
-    far_cols = far_cols.reshape(half * tokens, head_cols)
+    near_cols = near_cols.reshape(experts * tokens, head_cols)
+    far_cols = far_cols.reshape(experts * tokens, head_cols)
 
     keys = lax.all_gather(mem_keys, "mem", axis=0, tiled=True)
     values = lax.all_gather(mem_values, "mem", axis=0, tiled=True)
@@ -287,7 +300,7 @@
     ]
     w_down_grad = jnp.concatenate(down, axis=1)[None]
     side = my_half.astype(jnp.int32).reshape(1)
-    query_grad = attend(block_index, side, head_queries, near_cols, far_cols, keys, values)
+    query_grad = attend(block_index, side, near_cols, far_cols, tokens, keys, values)
     gate_grad, up_grad, combine_grad = slot_grads(
         side, near_rows, rows_a, rows_b, weights, gate_pre[0], up_pre[0], slot_weight
     )

time: 364 us -> 367 us (level)
  blocking collectives: 32.4 us -> 68.3 us
  local copies, waits for them, and re-layouts: 32.6 us -> 10.2 us
  waiting for transfers between devices: 178 us -> 166 us
  Pallas kernels: 52.2 us -> 60.7 us
    all_to_all x6 -> x4, waiting for transfers between devices: 85 us -> 35.3 us  [swap(): lax.all_to_all(rows, 'expert', split_axis=0, concat_axis=0, axis_index_gr...]
    ppermute x1 -> x3, waiting for transfers between devices: 46.1 us -> 89.6 us  [the longest x1 45.9 us: per_device(): lax.ppermute(after(jnp.where(upper, low_q, high_q), far_b), 'expert', par...]
    all_to_all x0 -> x1, blocking collectives: none -> 23.4 us  [swap(): lax.all_to_all(rows, 'expert', split_axis=0, concat_axis=0, axis_index_gr...]
    unnamed x38 -> x27, local copies, waits for them, and re-layouts: 27.3 us -> 6.6 us
    all_gather x1, blocking collectives: 32.4 us -> 44.9 us  [per_device(): lax.all_gather(after(packed, near_slots), 'expert', axis=0, tiled=False)]
    all_to_all x6 -> x4, starting transfers between devices: 26.2 us -> 19.5 us  [swap(): lax.all_to_all(rows, 'expert', split_axis=0, concat_axis=0, axis_index_gr...]
    ppermute x1, waiting for transfers between devices: 45.2 us -> 38.8 us  [per_device(): lax.ppermute(after(out_grad[:, part_cols:], far_a), 'expert', partner)]
    ppermute x1 -> x3, starting transfers between devices: 2.04 us -> 7.92 us  [the longest x1 4.13 us: per_device(): far_routes = lax.ppermute(routes_t, 'expert', partner)]
  transfers between devices with their start and end apart: 13 -> 13, of which waited for: 7 -> 6; matrix products, arithmetic and copies ran while one was open for 10% -> 6% of each run, Pallas kernels for 14% -> 17%
where the time goes in v3:
time: 367 us; the launch traced here: 366 us
  waiting for transfers between devices  166 us (45%)
  blocking collectives  68.3 us (19%)
  Pallas kernels  60.7 us (17%)
  starting transfers between devices  27.5 us (7%)
  other arithmetic  14.2 us (4%)
  between operations  14 us (4%)
  local copies, waits for them, and re-layouts  10.2 us (3%)
  matrix products  5.37 us (1%)
    ppermute x1, waiting for transfers between devices, per_device(): lax.ppermute(after(jnp.where(upper, low_q, high_q), far_b), 'expert', par...  45.9 us
    all_gather x1, blocking collectives, per_device(): lax.all_gather(after(packed, near_slots), 'expert', axis=0, tiled=False)  44.9 us
    ppermute x1, waiting for transfers between devices, per_device(): lax.ppermute(after(out_grad[:, :part_cols], far_routes), 'expert', partner)  42.2 us
    ppermute x1, waiting for transfers between devices, per_device(): lax.ppermute(after(out_grad[:, part_cols:], far_a), 'expert', partner)  38.8 us
    all_to_all x4, waiting for transfers between devices, swap(): lax.all_to_all(rows, 'expert', split_axis=0, concat_axis=0, axis_index_gr...  35.3 us
    pallas_call x1, Pallas kernels, attend(): pl.pallas_call(attend_kernel, out_shape=jax.ShapeDtypeStruct((rows, width...  33.2 us
    all_to_all x1, blocking collectives, swap(): lax.all_to_all(rows, 'expert', split_axis=0, concat_axis=0, axis_index_gr...  23.4 us
    all_to_all x4, starting transfers between devices, swap(): lax.all_to_all(rows, 'expert', split_axis=0, concat_axis=0, axis_index_gr...  19.5 us
  transfers between devices with their start and end apart: 13, of which 6 were waited for; matrix products, arithmetic and copies ran while one was open for 6% of the time, Pallas kernels for 17%

profile of v3, /device:TPU:0, one launch (start us, length us, event | category | flops | bytes accessed | tf_op | source)
XLA Modules:
  0.0 366.2 jit_solution(12583781241408802983)
XLA Ops:
  7.2 0.7 all-gather.10.cloned.1.call-update
  8.0 0.7 all-gather.6.cloned.1.call-update
  8.7 4.1 %collective-permute-start = (s32[2,256]{1,0:T(2,128)S(1)}, s32[2,256]{1,0:T(2,128)S(1)}, u32[]{:S(2)}, u32[]{:S(2)}) collective-permute-start(s32[2,256]{1,0:T(2,128)S(1)} %bitcast.93), channel_id=1, source_target_pairs={{0,4},{1,5},{2,6},{3,7},{4,0},{5,1},{6,2},{7,3},{8,12},{9,13},{10,... | collective-permute-start | bytes 6152 | tf_op jit(solution)/shard_map/ppermute | solution.py:224
  12.9 1.5 collective-permute-done
  14.5 0.2 fusion.13
  14.6 0.1 fusion.15
  14.8 0.2 fusion.9
  15.0 2.6 convolution_convert_fusion
  17.6 4.1 %all-to-all-start = ((bf16[4,96,4096]{2,1,0:T(8,128)(2,1)}), bf16[4,96,4096]{2,1,0:T(8,128)(2,1)S(1)}, u32[]{:S(2)}, u32[]{:S(2)}) async-start(bf16[4,96,4096]{2,1,0:T(8,128)(2,1)} %bitcast.83), calls=%async_computation | async-start | bytes 6291456 | tf_op jit(solution)/shard_map/all_to_all | solution.py:230
  21.7 0.7 all-gather.8.cloned.1.call-update
  22.5 3.0 broadcast_select_fusion.1
  25.5 1.5 fusion.31
  27.0 0.2 slice_bitcast_fusion.11
  27.2 1.4 maximum_maximum_fusion
  28.6 28.3 %all-to-all-done = bf16[4,96,4096]{2,1,0:T(8,128)(2,1)S(1)} async-done(((bf16[4,96,4096]{2,1,0:T(8,128)(2,1)}), bf16[4,96,4096]{2,1,0:T(8,128)(2,1)S(1)}, u32[]{:S(2)}, u32[]{:S(2)}) %all-to-all-start) | async-done | bytes 3145760 | tf_op jit(solution)/shard_map/all_to_all | solution.py:230
  56.9 4.4 %all-to-all-start.1 = ((bf16[4,512,512]{2,1,0:T(8,128)(2,1)}), bf16[4,512,512]{2,1,0:T(8,128)(2,1)}, u32[]{:S(2)}, u32[]{:S(2)}) async-start(bf16[4,512,512]{2,1,0:T(8,128)(2,1)} %maximum_maximum_fusion), calls=%async_computation.1 | async-start | bytes 4194304 | tf_op jit(solution)/shard_map/all_to_all | solution.py:230
  61.3 2.7 collective-permute-start.1
  64.0 42.2 %collective-permute-done.1 = bf16[256,2048]{1,0:T(8,128)(2,1)S(1)} collective-permute-done((bf16[256,2048]{1,0:T(8,128)(2,1)}, bf16[256,2048]{1,0:T(8,128)(2,1)S(1)}, u32[]{:S(2)}, u32[]{:S(2)}) %collective-permute-start.1) | collective-permute-done | bytes 1048608 | tf_op jit(solution)/shard_map/ppermute | solution.py:235
  106.2 1.0 copy-done.5
  107.3 1.7 convolution_convert_fusion.1
  109.0 7.0 %all-to-all-start.2 = ((bf16[4,96,2048]{2,1,0:T(8,128)(2,1)}), bf16[4,96,2048]{2,1,0:T(8,128)(2,1)S(1)}, u32[]{:S(2)}, u32[]{:S(2)}) async-start(bf16[4,96,2048]{2,1,0:T(8,128)(2,1)} %bitcast.84), calls=%async_computation.2 | async-start | bytes 3145728 | tf_op jit(solution)/shard_map/all_to_all | solution.py:230
  116.0 44.9 %all-gather.1 = f32[8,4,256]{2,1,0:T(4,128)S(1)} all-gather(f32[1,4,256]{2,1,0:T(4,128)S(1)} %bitcast.92), channel_id=2, replica_groups=mesh['mem'=4,'expert'=8] {'expert'}, dimensions={0}, use_global_device_ids=true | all-gather | bytes 36864 | tf_op jit(solution)/shard_map/all_gather | solution.py:263
  161.0 0.1 fusion.11
  161.1 0.3 select_reduce_fusion
  161.5 2.0 fusion.5
  163.6 0.3 fusion.6
  163.9 1.5 copy.27.wt_ref
  165.4 1.1 copy-done.4
  166.5 6.6 %shard_map.138 = bf16[768,2048]{1,0:T(8,128)(2,1)} custom-call(bf16[768,768]{1,0:T(8,128)(2,1)} %copy.27.wt_ref, bf16[384,4096]{1,0:T(8,128)(2,1)} %bitcast.78, bf16[384,2048]{1,0:T(8,128)(2,1)} %bitcast.86), custom_call_target="tpu_custom_call" | custom-call | flops 2415919104 | bytes 7471104 | tf_op jit(solution)/shard_map/pallas_call | solution.py:93
  173.1 1.1 copy-done.9
  174.3 38.8 %collective-permute-done.2 = bf16[256,2048]{1,0:T(8,128)(2,1)S(1)} collective-permute-done((bf16[256,2048]{1,0:T(8,128)(2,1)S(1)}, bf16[256,2048]{1,0:T(8,128)(2,1)S(1)}, u32[]{:S(2)}, u32[]{:S(2)}) %collective-permute-start.2) | collective-permute-done | bytes 1048608 | tf_op jit(solution)/shard_map/ppermute | solution.py:236
  213.1 0.6 convolution_convert_fusion.2
  213.7 23.4 %all_to_all.25 = bf16[4,96,2048]{2,1,0:T(8,128)(2,1)} all-to-all(bf16[4,96,2048]{2,1,0:T(8,128)(2,1)S(1)} %bitcast.85), channel_id=1, replica_groups={{0,1,2,3},{4,5,6,7},{8,9,10,11},{12,13,14,15},{16,17,18,19},{20,21,22,2..., dimensions={0} | all-to-all | bytes 3145728 | tf_op jit(solution)/shard_map/all_to_all | solution.py:230
  237.1 6.6 %shard_map.139 = bf16[768,2048]{1,0:T(8,128)(2,1)} custom-call(bf16[768,768]{1,0:T(8,128)(2,1)} %copy.27.wt_ref, bf16[384,4096]{1,0:T(8,128)(2,1)} %bitcast.79, bf16[384,2048]{1,0:T(8,128)(2,1)} %bitcast.88), custom_call_target="tpu_custom_call" | custom-call | flops 2415919104 | bytes 7471104 | tf_op jit(solution)/shard_map/pallas_call | solution.py:93
  243.7 1.2 copy-done.8
  244.9 1.1 collective-permute-start.3
  246.2 45.9 %collective-permute-done.3 = bf16[256,2048]{1,0:T(8,128)(2,1)S(1)} collective-permute-done((bf16[256,2048]{1,0:T(8,128)(2,1)S(1)}, bf16[256,2048]{1,0:T(8,128)(2,1)S(1)}, u32[]{:S(2)}, u32[]{:S(2)}) %collective-permute-start.3) | collective-permute-done | bytes 1048608 | tf_op jit(solution)/shard_map/ppermute | solution.py:250
  292.3 1.4 maximum_maximum_fusion.1
  293.7 3.9 %all-to-all-start.4 = ((bf16[4,512,512]{2,1,0:T(8,128)(2,1)}), bf16[4,512,512]{2,1,0:T(8,128)(2,1)S(1)}, u32[]{:S(2)}, u32[]{:S(2)}) async-start(bf16[4,512,512]{2,1,0:T(8,128)(2,1)} %maximum_maximum_fusion.1), calls=%async_computation.4 | async-start | bytes 4194304 | tf_op jit(solution)/shard_map/all_to_all | solution.py:230
  297.6 0.7 copy.26.idx_ref
  298.3 1.0 reshape.80.sw_ref
  299.3 14.3 %shard_map.140 = (bf16[768,768]{1,0:T(8,128)(2,1)}, bf16[768,768]{1,0:T(8,128)(2,1)}, f32[768,1]{1,0:T(8,128)}) custom-call(s32[1]{0:T(128)} %bitcast.half_ref, bf16[384,4096]{1,0:T(8,128)(2,1)} %bitcast.80, bf16[384,2048]{1,0:T(8,128)(2,1)} %bitcast.87, bf16[384,2048]{1,0:T(8,128)(2,1)} %bitcast.89, bf16[768,4096]{1,0:T(8,128)(2,1)} %bitcast.95, ...), custom_call_target="tpu_custom_call" | custom-call | flops 4831838208 | bytes 17301504 | tf_op jit(solution)/shard_map/pallas_call | solution.py:154
  313.7 1.2 reduce
  314.8 0.6 reshape.75
  315.4 6.9 %all-to-all-done.4 = bf16[4,512,512]{2,1,0:T(8,128)(2,1)S(1)} async-done(((bf16[4,512,512]{2,1,0:T(8,128)(2,1)}), bf16[4,512,512]{2,1,0:T(8,128)(2,1)S(1)}, u32[]{:S(2)}, u32[]{:S(2)}) %all-to-all-start.4) | async-done | bytes 2097184 | tf_op jit(solution)/shard_map/all_to_all | solution.py:230
  322.4 1.3 copy-done.1
  323.7 33.2 %shard_map.137 = bf16[2048,512]{1,0:T(8,128)(2,1)} custom-call(s32[16,4]{1,0:T(8,128)} %copy.26.idx_ref, s32[1]{0:T(128)} %bitcast.half_ref, bf16[2048,512]{1,0:T(8,128)(2,1)} %bitcast.13.nq_ref.near_ref, bf16[2048,512]{1,0:T(8,128)(2,1)} %bitcast.81, bf16[2048,512]{1,0:T(8,128)(2,1)} %bitcast.13.nq_ref.near_ref, bf16[2048,512]{1,0:T(8,128)(2,1)} %bitcast.82, ...), custom_call_target="tpu_custom_call" | custom-call | flops 3221225472 | bytes 14680064 | tf_op jit(solution)/shard_map/pallas_call | solution.py:52
  357.0 2.7 maximum_bitcast_fusion
  (50 shorter events, 0.9 us)
Async XLA Ops:
  7.2 1.5 copy-start.10
  7.2 7.8 %copy-start.2 = (bf16[256,4096]{1,0:T(8,128)(2,1)S(1)}, bf16[256,4096]{1,0:T(8,128)(2,1)}, u32[]{:S(2)}) copy-start(bf16[256,4096]{1,0:T(8,128)(2,1)} %param.11) | copy-start | bytes 6291460
  7.2 292.1 %all-gather.10.cloned.1.call-start = ((), (), s32[]{:S(2)}) async-start(), calls=%async_computation.11 | async-start | bytes 7864320 | tf_op jit(solution)/shard_map/all_gather | solution.py:279
  7.9 307.5 %all-gather.6.cloned.1.call-start = ((), (), s32[]{:S(2)}) async-start(), calls=%async_computation.7 | async-start | bytes 5242880 | tf_op jit(solution)/shard_map/all_gather | solution.py:277
  8.7 5.7 %collective-permute-start = (s32[2,256]{1,0:T(2,128)S(1)}, s32[2,256]{1,0:T(2,128)S(1)}, u32[]{:S(2)}, u32[]{:S(2)}) collective-permute-start(s32[2,256]{1,0:T(2,128)S(1)} %bitcast.93), channel_id=1, source_target_pairs={{0,4},{1,5},{2,6},{3,7},{4,0},{5,1},{6,2},{7,3},{8,12},{9,13},{10,... | collective-permute-start | bytes 6152 | tf_op jit(solution)/shard_map/ppermute | solution.py:224
  17.6 39.3 %all-to-all-start = ((bf16[4,96,4096]{2,1,0:T(8,128)(2,1)}), bf16[4,96,4096]{2,1,0:T(8,128)(2,1)S(1)}, u32[]{:S(2)}, u32[]{:S(2)}) async-start(bf16[4,96,4096]{2,1,0:T(8,128)(2,1)} %bitcast.83), calls=%async_computation | async-start | bytes 6291456 | tf_op jit(solution)/shard_map/all_to_all | solution.py:230
  21.7 293.7 %all-gather.8.cloned.1.call-start = ((), (), s32[]{:S(2)}) async-start(), calls=%async_computation.8 | async-start | bytes 5242880 | tf_op jit(solution)/shard_map/all_gather | solution.py:278
  22.5 3.0 copy-start.3
  56.9 52.1 %copy-start = (bf16[4,96,4096]{2,1,0:T(8,128)(2,1)}, bf16[4,96,4096]{2,1,0:T(8,128)(2,1)S(1)}, u32[]{:S(2)}) copy-start(bf16[4,96,4096]{2,1,0:T(8,128)(2,1)S(1)} %all-to-all-done) | copy-start | bytes 9437188
  56.9 52.1 %all-to-all-start.1 = ((bf16[4,512,512]{2,1,0:T(8,128)(2,1)}), bf16[4,512,512]{2,1,0:T(8,128)(2,1)}, u32[]{:S(2)}, u32[]{:S(2)}) async-start(bf16[4,512,512]{2,1,0:T(8,128)(2,1)} %maximum_maximum_fusion), calls=%async_computation.1 | async-start | bytes 4194304 | tf_op jit(solution)/shard_map/all_to_all | solution.py:230
  61.3 44.9 %collective-permute-start.1 = (bf16[256,2048]{1,0:T(8,128)(2,1)}, bf16[256,2048]{1,0:T(8,128)(2,1)S(1)}, u32[]{:S(2)}, u32[]{:S(2)}) collective-permute-start(bf16[256,2048]{1,0:T(8,128)(2,1)} %get-tuple-element.17), channel_id=1, source_target_pairs={{0,4},{1,5},{2,6},{3,7},{4,0},{5,1},{6,2},{7,3},{8,12},{9,13},{10,... | collective-permute-start | bytes 3145736 | tf_op jit(solution)/shard_map/ppermute | solution.py:235
  106.2 1.0 copy-start.5
  107.3 8.7 %copy-start.12 = (bf16[256,2]{0,1:T(2,128)(2,1)S(1)}, bf16[256,2]{0,1:T(2,128)(2,1)}, u32[]{:S(2)}) copy-start(bf16[256,2]{0,1:T(2,128)(2,1)} %param.16) | copy-start | bytes 3076
  109.0 52.5 %copy-start.7 = (bf16[1,768,768]{2,1,0:T(8,128)(2,1)S(1)}, bf16[1,768,768]{2,1,0:T(8,128)(2,1)}, u32[]{:S(2)}) copy-start(bf16[1,768,768]{2,1,0:T(8,128)(2,1)} %param.18) | copy-start | bytes 3538948
  109.0 56.3 %all-to-all-start.2 = ((bf16[4,96,2048]{2,1,0:T(8,128)(2,1)}), bf16[4,96,2048]{2,1,0:T(8,128)(2,1)S(1)}, u32[]{:S(2)}, u32[]{:S(2)}) async-start(bf16[4,96,2048]{2,1,0:T(8,128)(2,1)} %bitcast.84), calls=%async_computation.2 | async-start | bytes 3145728 | tf_op jit(solution)/shard_map/all_to_all | solution.py:230
  116.0 241.0 %reduce-scatter.3.cloned.1.call-start = ((), (), s32[]{:S(2)}) async-start(), calls=%async_computation.9 | async-start | bytes 3932160 | tf_op jit(solution)/shard_map/reduce_scatter | solution.py:296
  165.4 1.1 copy-start.4
  173.1 1.2 copy-start.9
  173.1 183.9 %reduce-scatter.5.cloned.1.call-start = ((), (), s32[]{:S(2)}) async-start(), calls=%async_computation.10 | async-start | bytes 3932160 | tf_op jit(solution)/shard_map/reduce_scatter | solution.py:296
  174.3 38.8 %collective-permute-start.2 = (bf16[256,2048]{1,0:T(8,128)(2,1)S(1)}, bf16[256,2048]{1,0:T(8,128)(2,1)S(1)}, u32[]{:S(2)}, u32[]{:S(2)}) collective-permute-start(bf16[256,2048]{1,0:T(8,128)(2,1)S(1)} %copy-done.9), channel_id=1, source_target_pairs={{0,4},{1,5},{2,6},{3,7},{4,0},{5,1},{6,2},{7,3},{8,12},{9,13},{10,... | collective-permute-start | bytes 3145736 | tf_op jit(solution)/shard_map/ppermute | solution.py:236
  243.7 1.2 copy-start.8
  243.7 2.3 copy-start.6
  244.9 47.2 %collective-permute-start.3 = (bf16[256,2048]{1,0:T(8,128)(2,1)S(1)}, bf16[256,2048]{1,0:T(8,128)(2,1)S(1)}, u32[]{:S(2)}, u32[]{:S(2)}) collective-permute-start(bf16[256,2048]{1,0:T(8,128)(2,1)S(1)} %copy-done.8), channel_id=1, source_target_pairs={{0,4},{1,5},{2,6},{3,7},{4,0},{5,1},{6,2},{7,3},{8,12},{9,13},{10,... | collective-permute-start | bytes 3145736 | tf_op jit(solution)/shard_map/ppermute | solution.py:250
  293.7 3.9 %copy-start.11 = (s32[16,4]{0,1:T(4,128)S(1)}, s32[16,4]{0,1:T(4,128)}, u32[]{:S(2)}) copy-start(s32[16,4]{0,1:T(4,128)} %param.14) | copy-start | bytes 772
  293.7 28.7 %all-to-all-start.4 = ((bf16[4,512,512]{2,1,0:T(8,128)(2,1)}), bf16[4,512,512]{2,1,0:T(8,128)(2,1)S(1)}, u32[]{:S(2)}, u32[]{:S(2)}) async-start(bf16[4,512,512]{2,1,0:T(8,128)(2,1)} %maximum_maximum_fusion.1), calls=%async_computation.4 | async-start | bytes 4194304 | tf_op jit(solution)/shard_map/all_to_all | solution.py:230
  322.4 1.3 copy-start.1
Sparse Core Ops, SparseCore 0:
  9.6 49.0 all-gather.9
  60.2 34.4 all-gather.5
  96.3 34.4 all-gather.7
  173.2 34.9 reduce-scatter.2
  243.9 35.7 reduce-scatter.4
